TPU v7x, 32 devices: a whole 2x2x4 slice. The times are simulated.
32 devices in a mesh: groups: 2 (over x), neuron: 16 (over z, y, core).
Axes of the slice: x: 2, y: 2, z: 4, core: 2. Of those that a mesh axis runs over, the one named last changes fastest.
Arguments:
- queries: bfloat16 [1024, 8, 128], P(('groups', 'neuron')), parts along dimension 0, may hold values from -18 to 18
- keys: bfloat16 [1024, 1024, 128], P(('groups', 'neuron')), parts along dimension 0, may hold values from -6 to 6
- values: bfloat16 [1024, 1024, 128], P(('groups', 'neuron')), parts along dimension 0, may hold values from -6 to 6
- lengths: int32 [256], P('groups'), parts along dimension 0, may hold values from 256 to 1024
- active_blocks: int32 [32, 32], P('groups'), parts along dimension 0, may hold values from 0 to 111, all different within a row
- residual: bfloat16 [256, 4096], P('groups', 'neuron'), parts along dimension 0, may hold values from -18 to 18
- out_weight: bfloat16 [4096, 4096], P(None, 'neuron'), may hold values from -0.09375 to 0.09375
- norm_gain: bfloat16 [4096], P('neuron'), may hold values from 0.099609375 to 1.8984375
- gate_weight: bfloat16 [4096, 14336], P('neuron'), may hold values from -0.09375 to 0.09375
- up_weight: bfloat16 [4096, 14336], P('neuron'), may hold values from -0.09375 to 0.09375
- down_weight: bfloat16 [14336, 4096], P(None, 'neuron'), may hold values from -0.09375 to 0.09375
Outputs:
- layer_out: bfloat16 [256, 4096], P('groups', 'neuron'), parts along dimension 0
There are 2 independent parts, one for each index of `groups`. A program takes and returns all parts, laid end to end along the dimension named above; an argument that names none is the same for every part. Nothing has to cross between parts.
Inputs may be any that keep to these rules, and one draw needn't show every extreme that they name: `active_blocks`: each row names 32 different blocks; every block is named by some row.
All inputs are finite; a program needn't handle non-finite values.
Results may differ from a plain program's by a relative error of at most 0.0052.
Values may be sent and summed in bfloat16 or wider, within the bound.
A program may use at most 128 MiB of HBM per device.

v0:
```python
import jax
import jax.numpy as jnp
from jax import lax
from jax.sharding import PartitionSpec as P

D = 4096
BLK = 128
ROWS = 128


def whole_attention(queries, keys, values, live_lengths, score_scale):
    scores = (
        jnp.einsum("egc,etc->egt", queries, keys, preferred_element_type=jnp.float32) * score_scale
    )
    live_mask = (
        jnp.arange(keys.shape[1], dtype=jnp.int32)[None, None, :] < live_lengths[:, None, None]
    )
    scores = jnp.where(live_mask, scores, -1e30)
    running_max = jnp.max(scores, axis=-1, keepdims=True)
    weights = jnp.where(live_mask, jnp.exp(scores - running_max), 0.0)
    probs = (weights / jnp.sum(weights, axis=-1, keepdims=True)).astype(jnp.bfloat16)
    return jnp.einsum("egt,etc->egc", probs, values, preferred_element_type=jnp.float32).astype(
        jnp.bfloat16
    )


def body(
    queries,
    keys,
    values,
    lengths,
    active_blocks,
    residual,
    out_weight,
    norm_gain,
    gate_weight,
    up_weight,
    down_weight,
):
    entries = keys.shape[0]
    first_entry = lax.axis_index("neuron") * entries
    row_start = first_entry % ROWS
    live_lengths = lax.dynamic_slice_in_dim(lengths, row_start, entries)
    score_scale = queries.shape[2] ** (-0.5)
    attended = whole_attention(queries, keys, values, live_lengths, score_scale)
    attended = attended.reshape(entries, -1)
    gathered = lax.all_gather(attended, "neuron", axis=0, tiled=True)
    by_head = gathered.reshape(gathered.shape[0] // ROWS, ROWS, gathered.shape[1])
    out_heads = out_weight.reshape(by_head.shape[0], by_head.shape[2], out_weight.shape[1])
    stream = residual.astype(jnp.float32) + jnp.einsum(
        "hrc,hcd->rd", by_head, out_heads, preferred_element_type=jnp.float32
    )
    square_sums = lax.psum(jnp.sum(stream * stream, axis=1), "neuron")
    normed = (
        stream * lax.rsqrt(square_sums / D + 1e-05)[:, None] * norm_gain.astype(jnp.float32)
    ).astype(jnp.bfloat16)
    num_groups = active_blocks.shape[0]
    group_rows = ROWS // num_groups
    local_width = gate_weight.shape[0]
    gate_blocks = gate_weight.reshape(local_width, -1, BLK)
    up_blocks = up_weight.reshape(local_width, -1, BLK)
    down_blocks = down_weight.reshape(-1, BLK, down_weight.shape[1])

    def project_up(operand):
        rows_in, picked = operand
        gate_cols = jnp.take(gate_blocks, picked, axis=1).reshape(local_width, -1)
        up_cols = jnp.take(up_blocks, picked, axis=1).reshape(local_width, -1)
        return (
            jnp.dot(rows_in, gate_cols, preferred_element_type=jnp.float32),
            jnp.dot(rows_in, up_cols, preferred_element_type=jnp.float32),
        )

    gate_part, up_part = lax.map(
        project_up, (normed.reshape(num_groups, group_rows, local_width), active_blocks)
    )
    gate_part = gate_part.reshape(ROWS, -1)
    up_part = up_part.reshape(ROWS, -1)
    gate_total, up_total = lax.psum((gate_part, up_part), "neuron")
    activated = (jnp.maximum(gate_total, 0.0) * up_total).astype(jnp.bfloat16)

    def project_down(operand):
        rows_in, picked = operand
        down_rows = jnp.take(down_blocks, picked, axis=0).reshape(-1, down_blocks.shape[2])
        return jnp.dot(rows_in, down_rows, preferred_element_type=jnp.float32)

    down_part = lax.map(
        project_down, (activated.reshape(num_groups, group_rows, -1), active_blocks)
    )
    return (stream + down_part.reshape(ROWS, -1)).astype(jnp.bfloat16)


def solution(mesh):
    in_specs = (
        P(("groups", "neuron"), None, None),
        P(("groups", "neuron"), None, None),
        P(("groups", "neuron"), None, None),
        P("groups"),
        P("groups", None),
        P("groups", "neuron"),
        P(None, "neuron"),
        P("neuron"),
        P("neuron", None),
        P("neuron", None),
        P(None, "neuron"),
    )
    out_specs = P("groups", "neuron")
    return jax.shard_map(body, mesh=mesh, in_specs=in_specs, out_specs=out_specs, check_vma=False)
```

profile of v0, /device:TPU:0, one launch (start us, length us, event | category | flops | bytes accessed | tf_op | source)
XLA Modules:
  0.0 679.0 jit_solution(18427705896115794409)
XLA Ops:
  7.5 5.0 fusion.24
  12.5 4.6 convolution_convert_fusion
  17.9 10.1 %copy.14 = bf16[256,14336]{0,1:T(8,128)(2,1)} copy(bf16[256,14336]{1,0:T(8,128)(2,1)} %param.25) | data formatting | bytes 14680064 | tf_op args[8]
  28.0 10.4 %copy.16 = bf16[256,112,128]{2,0,1:T(8,128)(2,1)} copy(bf16[256,112,128]{0,2,1:T(8,128)(2,1)} %bitcast.105) | data formatting | bytes 14680064 | tf_op jit(solution)/shard_map/while | solution.py:73
  38.5 10.5 %copy.15 = bf16[256,14336]{0,1:T(8,128)(2,1)} copy(bf16[256,14336]{1,0:T(8,128)(2,1)} %param.26) | data formatting | bytes 14680064 | tf_op args[9]
  48.9 10.3 %copy.17 = bf16[256,112,128]{2,0,1:T(8,128)(2,1)} copy(bf16[256,112,128]{0,2,1:T(8,128)(2,1)} %bitcast.106) | data formatting | bytes 14680064 | tf_op jit(solution)/shard_map/while | solution.py:73
  61.0 34.8 %psum.21 = f32[128]{0:T(128)S(1)} all-reduce(f32[128]{0:T(128)S(1)} %get-tuple-element.113), channel_id=1, replica_groups=mesh['groups'=2,'neuron'=16] {'neuron'}, use_global_device_ids=true, to_apply=%region_3.4 | all-reduce | flops 128 | bytes 1024 | tf_op jit(solution)/shard_map/psum | solution.py:53
  95.9 370.0 %while.22 = (s32[]{:T(128)}, f32[16,8,4096]{2,1,0:T(8,128)}, f32[16,8,4096]{2,1,0:T(8,128)}, bf16[16,8,256]{2,1,0:T(8,128)(2,1)S(1)}, s32[16,32]{1,0:T(8,128)}, ...) while((s32[]{:T(128)}, f32[16,8,4096]{2,1,0:T(8,128)}, ...), condition=%wide.region_5.7_spmd, body=%wide.region_4.6_spmd.sunk | while | flops 35652800 | bytes 29637400 | solution.py:73
  96.6 4.0 gather_fusion
  100.7 5.2 gather_fusion.1
  119.7 4.0 gather_fusion
  123.8 5.2 gather_fusion.1
  129.0 4.0 select_bitcast_fusion.3
  142.9 4.0 gather_fusion
  146.9 5.2 gather_fusion.1
  166.0 4.0 gather_fusion
  170.0 5.2 gather_fusion.1
  175.3 4.0 select_bitcast_fusion.3
  189.1 4.0 gather_fusion
  193.2 5.2 gather_fusion.1
  212.2 4.0 gather_fusion
  216.3 5.2 gather_fusion.1
  235.4 4.0 gather_fusion
  239.4 5.2 gather_fusion.1
  258.5 4.0 gather_fusion
  262.6 5.2 gather_fusion.1
  281.7 4.0 gather_fusion
  285.7 5.2 gather_fusion.1
  290.9 4.0 select_bitcast_fusion.3
  304.8 4.0 gather_fusion
  308.8 5.2 gather_fusion.1
  314.1 4.0 select_bitcast_fusion.3
  327.9 4.0 gather_fusion
  331.9 5.2 gather_fusion.1
  337.2 4.0 select_bitcast_fusion.3
  351.0 4.0 gather_fusion
  355.1 5.2 gather_fusion.1
  374.1 4.0 gather_fusion
  378.2 5.2 gather_fusion.1
  397.3 4.0 gather_fusion
  401.3 5.2 gather_fusion.1
  420.4 4.0 gather_fusion
  424.4 5.2 gather_fusion.1
  429.7 4.0 select_bitcast_fusion.3
  443.5 4.0 gather_fusion
  447.6 5.2 gather_fusion.1
  466.0 108.6 %all-reduce.3.cloned.1.call-done = (f32[128,4096]{1,0:T(8,128)}, f32[128,4096]{1,0:T(8,128)}) async-done(((f32[128,4096]{1,0:T(8,128)}, f32[128,4096]{1,0:T(8,128)}), (f32[128,4096]{1,0:T(8,128)}, f32[128,4096]{1,0:T(8,128)})) %all-reduce.3.cloned.1.call-update) | async-done | bytes 4194320 | tf_op jit(solution)/shard_map/psum | solution.py:78
  577.1 93.5 %while.23 = (s32[]{:T(128)}, f32[16,8,256]{2,1,0:T(8,128)S(1)}, bf16[16,8,4096]{2,1,0:T(8,128)(2,1)S(1)}, s32[16,32]{1,0:T(8,128)}, bf16[112,128,256]{2,1,0:T(8,128)(2,1)}, /*index=5*/s32[]{:T(128)}) while((s32[]{:T(128)}, f32[16,8,256]{2,1,0:T(8,128)S(1)}, bf16[16,8,4096]{2,1,0:T(8,128)(2,1)S(1)}, s32[16,32]{1,0:T(8,128)}, ...), condition=%wide.region_9.11_spmd, body=%wide.region_8.10_spmd.sunk | while | flops 17827104 | bytes 10565389 | solution.py:86
  (227 shorter events, 298.3 us)
Async XLA Ops:
  6.5 52.7 %copy-start = (bf16[4096,256]{1,0:T(8,128)(2,1)S(1)}, bf16[4096,256]{1,0:T(8,128)(2,1)}, u32[]{:S(2)}) copy-start(bf16[4096,256]{1,0:T(8,128)(2,1)} %param.23) | copy-start | bytes 6291460
  6.5 52.7 %all-gather.2.cloned.1.call-start = ((), (), s32[]{:S(2)}) async-start(), calls=%async_computation | async-start | bytes 1114112 | tf_op jit(solution)/shard_map/all_gather | solution.py:47
  12.5 5.4 copy-start.3
  17.8 556.8 %all-reduce.3.cloned.1.call-start = ((), (), s32[]{:S(2)}) async-start(), calls=%async_computation.1 | async-start | bytes 8388608 | tf_op jit(solution)/shard_map/psum | solution.py:78
  48.9 10.3 %copy-start.2 = (bf16[128,256]{1,0:T(8,128)(2,1)S(1)}, bf16[128,256]{1,0:T(8,128)(2,1)}, u32[]{:S(2)}) copy-start(bf16[128,256]{1,0:T(8,128)(2,1)} %param.22) | copy-start | bytes 196612
  670.5 1.6 copy-start.1
Sparse Core Ops, SparseCore 0:
  17.9 40.5 all-gather.1
  466.1 108.4 all-reduce.2
where the time goes:
time: 686 us; the launch traced here: 679 us
  local copies, waits for them, and re-layouts  357 us (52%)
  waiting for transfers between devices  109 us (16%)
  other arithmetic  105 us (15%)
  matrix products  59.3 us (9%)
  blocking collectives  34.8 us (5%)
  between operations  13.5 us (2%)
    psum x1, waiting for transfers between devices, body(): gate_total, up_total = lax.psum((gate_part, up_part), 'neuron')  109 us
    gather x16, local copies, waits for them, and re-layouts, project_up(): gate_cols = jnp.take(gate_blocks, picked, axis=1).reshape(local_width, -1)  83.7 us
    gather x16, local copies, waits for them, and re-layouts, project_up(): up_cols = jnp.take(up_blocks, picked, axis=1).reshape(local_width, -1)  64.5 us
    select_n x16, other arithmetic, project_up(): up_cols = jnp.take(up_blocks, picked, axis=1).reshape(local_width, -1)  63.7 us
    gather x16, local copies, waits for them, and re-layouts, project_down(): jnp.take(down_blocks, picked, axis=0).reshape(-1, down_blocks.shape[2])  60.2 us
    select_n x16, local copies, waits for them, and re-layouts, project_up(): gate_cols = jnp.take(gate_blocks, picked, axis=1).reshape(local_width, -1)  52.3 us
    select_n x16, local copies, waits for them, and re-layouts, project_up(): up_cols = jnp.take(up_blocks, picked, axis=1).reshape(local_width, -1)  52.3 us
    psum x1, blocking collectives, body(): square_sums = lax.psum(jnp.sum(stream * stream, axis=1), 'neuron')  34.8 us
  transfers between devices with their start and end apart: 2, of which 1 were waited for; matrix products, arithmetic and copies ran while one was open for 6% of the time, Pallas kernels for 0%

commit v1 on v0

v1 whole, which is shorter than its diff:
```python
import functools

import jax
import jax.numpy as jnp
from jax import lax
from jax.experimental import pallas as pl
from jax.experimental.pallas import tpu as pltpu
from jax.sharding import PartitionSpec as P

AXIS = "neuron"
VMEM_LIMIT = 60 * 1024 * 1024


def fitting(total, most):
    size = most
    while total % size:
        size -= 1
    return size


def attention_kernel(lengths, q_ref, k_ref, v_ref, out_ref, held, few, *, per_step, rows):
    step = pl.program_id(0)
    entries, heads = out_ref.shape[0], q_ref.shape[1]
    width, slots = q_ref.shape[2], k_ref.shape[1]
    scale = width ** (-0.5)
    first = lax.rem(lax.axis_index(AXIS) * entries, rows)
    slot = lax.broadcasted_iota(jnp.int32, (heads, slots), 1)
    for i in range(per_step):
        e = step * per_step + i
        live = slot < lengths[first + e]
        scores = lax.dot_general(
            q_ref[i], k_ref[i], (((1,), (1,)), ((), ())), preferred_element_type=jnp.float32
        )
        scores = jnp.where(live, scores * scale, -1e30)
        top = jnp.max(scores, axis=1, keepdims=True)
        weights = jnp.where(live, jnp.exp(scores - top), 0.0)
        total = jnp.sum(weights, axis=1, keepdims=True)
        probs = (weights * (1.0 / total)).astype(jnp.bfloat16)
        mixed = jnp.dot(probs, v_ref[i], preferred_element_type=jnp.float32)
        for j in range(heads):
            few[i : i + 1, j * width : (j + 1) * width] = mixed[j : j + 1, :]
    held[pl.ds(pl.multiple_of(step * per_step, per_step), per_step), :] = few[...]

    @pl.when(step == pl.num_programs(0) - 1)
    def _():
        out_ref[...] = held[...].astype(out_ref.dtype)


def attention(queries, keys, values, lengths):
    entries, heads, width = queries.shape
    slots = keys.shape[1]
    per_step = fitting(entries, 8)
    return pl.pallas_call(
        functools.partial(attention_kernel, per_step=per_step, rows=lengths.shape[0]),
        out_shape=jax.ShapeDtypeStruct((entries, heads * width), jnp.bfloat16),
        grid_spec=pltpu.PrefetchScalarGridSpec(
            num_scalar_prefetch=1,
            grid=(entries // per_step,),
            in_specs=[
                pl.BlockSpec((per_step, heads, width), lambda s, n: (s, 0, 0)),
                pl.BlockSpec((per_step, slots, width), lambda s, n: (s, 0, 0)),
                pl.BlockSpec((per_step, slots, width), lambda s, n: (s, 0, 0)),
            ],
            out_specs=pl.BlockSpec((entries, heads * width), lambda s, n: (0, 0)),
            scratch_shapes=[
                pltpu.VMEM((entries, heads * width), jnp.float32),
                pltpu.VMEM((per_step, heads * width), jnp.float32),
            ],
        ),
        compiler_params=pltpu.CompilerParams(
            dimension_semantics=("arbitrary",), vmem_limit_bytes=VMEM_LIMIT
        ),
        name="attention",
    )(lengths, queries, keys, values)


def up_kernel(picked, x_ref, gate_ref, up_ref, out_ref, gate_all, up_all):
    step = pl.program_id(0)
    blk = gate_all.shape[2]
    per_step = gate_ref.shape[1] // blk
    groups, active = picked.shape
    group_rows = x_ref.shape[0] // groups
    x = x_ref[...]
    for pair in range(0, per_step, 2):
        n = min(2, per_step - pair)
        cols = slice(pair * blk, (pair + n) * blk)
        for w_ref, dense in ((gate_ref, gate_all), (up_ref, up_all)):
            part = jnp.dot(x, w_ref[:, cols], preferred_element_type=jnp.float32)
            for i in range(n):
                dense[step * per_step + pair + i] = part[:, i * blk : (i + 1) * blk]

    @pl.when(step == pl.num_programs(0) - 1)
    def _():
        @pl.loop(0, groups)
        def _(g):
            row = pl.multiple_of(g * group_rows, group_rows)
            for j in range(active):
                b = picked[g, j]
                both = jnp.concatenate(
                    [gate_all[b, pl.ds(row, group_rows), :], up_all[b, pl.ds(row, group_rows), :]],
                    axis=0,
                )
                out_ref[g * active + j] = both.astype(out_ref.dtype)


def project_up(normed, gate_weight, up_weight, picked, blk, out_type):
    rows, width = normed.shape
    ff = gate_weight.shape[1]
    blocks = ff // blk
    groups, active = picked.shape
    group_rows = rows // groups
    per_step = fitting(blocks, 16)
    return pl.pallas_call(
        up_kernel,
        out_shape=jax.ShapeDtypeStruct((groups * active, 2 * group_rows, blk), out_type),
        grid_spec=pltpu.PrefetchScalarGridSpec(
            num_scalar_prefetch=1,
            grid=(blocks // per_step,),
            in_specs=[
                pl.BlockSpec((rows, width), lambda s, n: (0, 0)),
                pl.BlockSpec((width, per_step * blk), lambda s, n: (0, s)),
                pl.BlockSpec((width, per_step * blk), lambda s, n: (0, s)),
            ],
            out_specs=pl.BlockSpec(
                (groups * active, 2 * group_rows, blk), lambda s, n: (0, 0, 0)
            ),
            scratch_shapes=[pltpu.VMEM((blocks, rows, blk), jnp.float32)] * 2,
        ),
        compiler_params=pltpu.CompilerParams(
            dimension_semantics=("arbitrary",), vmem_limit_bytes=VMEM_LIMIT
        ),
        name="project_up",
    )(picked, normed, gate_weight, up_weight)


def down_kernel(picked, act_ref, down_ref, stream_ref, out_ref, dense, total):
    step = pl.program_id(0)
    blk = dense.shape[2]
    per_step = down_ref.shape[0] // blk
    groups, active = picked.shape
    group_rows = dense.shape[1] // groups

    @pl.when(step == 0)
    def _():
        @pl.loop(0, dense.shape[0])
        def _(b):
            dense[b] = jnp.zeros(dense.shape[1:], jnp.float32)

        @pl.loop(0, groups)
        def _(g):
            row = pl.multiple_of(g * group_rows, group_rows)
            for j in range(0, active, 2):
                both = act_ref[(g * active + j) // 2].astype(jnp.float32)
                dense[picked[g, j], pl.ds(row, group_rows), :] = both[:group_rows]
                dense[picked[g, j + 1], pl.ds(row, group_rows), :] = both[group_rows:]

        total[...] = stream_ref[...]

    acc = total[...]
    for pair in range(0, per_step, 2):
        n = min(2, per_step - pair)
        lhs = jnp.concatenate(
            [dense[step * per_step + pair + i] for i in range(n)], axis=1
        ).astype(jnp.bfloat16)
        acc += jnp.dot(
            lhs, down_ref[pair * blk : (pair + n) * blk, :], preferred_element_type=jnp.float32
        )
    total[...] = acc

    @pl.when(step == pl.num_programs(0) - 1)
    def _():
        out_ref[...] = acc.astype(out_ref.dtype)


def project_down(activated, down_weight, stream, picked, blk):
    rows, width = stream.shape
    blocks = down_weight.shape[0] // blk
    per_step = fitting(blocks, 16)
    return pl.pallas_call(
        down_kernel,
        out_shape=jax.ShapeDtypeStruct((rows, width), jnp.bfloat16),
        grid_spec=pltpu.PrefetchScalarGridSpec(
            num_scalar_prefetch=1,
            grid=(blocks // per_step,),
            in_specs=[
                pl.BlockSpec(activated.shape, lambda s, n: (0, 0, 0)),
                pl.BlockSpec((per_step * blk, width), lambda s, n: (s, 0)),
                pl.BlockSpec((rows, width), lambda s, n: (0, 0)),
            ],
            out_specs=pl.BlockSpec((rows, width), lambda s, n: (0, 0)),
            scratch_shapes=[
                pltpu.VMEM((blocks, rows, blk), jnp.float32),
                pltpu.VMEM((rows, width), jnp.float32),
            ],
        ),
        compiler_params=pltpu.CompilerParams(
            dimension_semantics=("arbitrary",), vmem_limit_bytes=VMEM_LIMIT
        ),
        name="project_down",
    )(picked, activated, down_weight, stream)


BLK = 128


def body(
    queries,
    keys,
    values,
    lengths,
    active_blocks,
    residual,
    out_weight,
    norm_gain,
    gate_weight,
    up_weight,
    down_weight,
):
    rows = residual.shape[0]
    groups, active = active_blocks.shape
    group_rows = rows // groups
    members = lax.axis_size(AXIS)
    model = residual.shape[1] * members
    attended = attention(queries, keys, values, lengths)
    gathered = lax.all_gather(attended, AXIS, axis=0, tiled=True)
    by_head = gathered.reshape(gathered.shape[0] // rows, rows, gathered.shape[1])
    out_heads = out_weight.reshape(by_head.shape[0], by_head.shape[2], out_weight.shape[1])
    stream = residual.astype(jnp.float32) + jnp.einsum(
        "hrc,hcd->rd", by_head, out_heads, preferred_element_type=jnp.float32
    )
    square_sums = lax.psum(jnp.sum(stream * stream, axis=1), AXIS)
    normed = (
        stream * lax.rsqrt(square_sums / model + 1e-05)[:, None] * norm_gain.astype(jnp.float32)
    ).astype(jnp.bfloat16)
    parts = project_up(normed, gate_weight, up_weight, active_blocks, BLK, jnp.float32)
    mine = lax.psum_scatter(parts, AXIS, scatter_dimension=0, tiled=True)
    act = (jnp.maximum(mine[:, :group_rows], 0.0) * mine[:, group_rows:]).astype(jnp.bfloat16)
    act = act.reshape(act.shape[0] // 2, 2 * group_rows, act.shape[2])
    activated = lax.all_gather(act, AXIS, axis=0, tiled=True)
    return project_down(activated, down_weight, stream, active_blocks, BLK)


def solution(mesh):
    in_specs = (
        P(("groups", "neuron"), None, None),
        P(("groups", "neuron"), None, None),
        P(("groups", "neuron"), None, None),
        P("groups"),
        P("groups", None),
        P("groups", "neuron"),
        P(None, "neuron"),
        P("neuron"),
        P("neuron", None),
        P("neuron", None),
        P(None, "neuron"),
    )
    out_specs = P("groups", "neuron")
    return jax.shard_map(body, mesh=mesh, in_specs=in_specs, out_specs=out_specs, check_vma=False)
```

time: 686 us -> 237 us (0.35)
  local copies, waits for them, and re-layouts: 357 us -> 0.02 us
  other arithmetic: 105 us -> 2.35 us
  matrix products: 59.3 us -> 1.75 us
  waiting for transfers between devices: 109 us -> 148 us
  Pallas kernels: 0 us -> 38.9 us
    gather x48 -> x0, local copies, waits for them, and re-layouts: 208 us -> none  [the longest x16 83.7 us: project_up(): gate_cols = jnp.take(gate_blocks, picked, axis=1).reshape(local_width, -1)]
    psum x1 -> x0, waiting for transfers between devices: 109 us -> none  [body(): gate_total, up_total = lax.psum((gate_part, up_part), 'neuron')]
    select_n x32 -> x0, local copies, waits for them, and re-layouts: 105 us -> none  [the longest x16 52.3 us: project_up(): gate_cols = jnp.take(gate_blocks, picked, axis=1).reshape(local_width, -1)]
    select_n x48 -> x0, other arithmetic: 79.2 us -> none  [the longest x16 63.7 us: project_up(): up_cols = jnp.take(up_blocks, picked, axis=1).reshape(local_width, -1)]
    all_gather x1 -> x2, waiting for transfers between devices: 0.01 us -> 78.2 us  [the longest x1 40.7 us: body(): gathered = lax.all_gather(attended, AXIS, axis=0, tiled=True)]
    reduce_scatter x0 -> x1, waiting for transfers between devices: none -> 70.1 us  [body(): mine = lax.psum_scatter(parts, AXIS, scatter_dimension=0, tiled=True)]
    dot_general x49 -> x0, matrix products: 52.6 us -> none  [the longest x16 21 us: project_up(): jnp.dot(rows_in, up_cols, preferred_element_type=jnp.float32)]
    pallas_call x0 -> x3, Pallas kernels: none -> 38.9 us  [the longest x1 16.4 us: attention(): pl.pallas_call(functools.partial(attention_kernel, per_step=per_step, row...]
  transfers between devices with their start and end apart: 2 -> 3, of which waited for: 1 -> 3; matrix products, arithmetic and copies ran while one was open for 6% -> 0% of each run, Pallas kernels for 0% -> 0%
where the time goes in v1:
time: 237 us; the launch traced here: 236 us
  waiting for transfers between devices  148 us (62%)
  Pallas kernels  38.9 us (16%)
  blocking collectives  31.6 us (13%)
  between operations  13.1 us (6%)
    reduce_scatter x1, waiting for transfers between devices, body(): mine = lax.psum_scatter(parts, AXIS, scatter_dimension=0, tiled=True)  70.1 us
    all_gather x1, waiting for transfers between devices, body(): gathered = lax.all_gather(attended, AXIS, axis=0, tiled=True)  40.7 us
    all_gather x1, waiting for transfers between devices, body(): activated = lax.all_gather(act, AXIS, axis=0, tiled=True)  37.6 us
    psum x1, blocking collectives, body(): square_sums = lax.psum(jnp.sum(stream * stream, axis=1), AXIS)  31.6 us
    pallas_call x1, Pallas kernels, attention(): pl.pallas_call(functools.partial(attention_kernel, per_step=per_step, row...  16.4 us
    pallas_call x1, Pallas kernels, project_up(): pl.pallas_call(up_kernel, out_shape=jax.ShapeDtypeStruct((groups * active...  11.8 us
    pallas_call x1, Pallas kernels, project_down(): pl.pallas_call(down_kernel, out_shape=jax.ShapeDtypeStruct((rows, width),...  10.7 us
  transfers between devices with their start and end apart: 3, of which 3 were waited for; matrix products, arithmetic and copies ran while one was open for 0% of the time, Pallas kernels for 0%

profile of v1, /device:TPU:0, one launch (start us, length us, event | category | flops | bytes accessed | tf_op | source)
XLA Modules:
  0.0 236.2 jit_solution(13017069688290753799)
XLA Ops:
  6.5 0.0 copy-start
  6.5 0.0 copy-start.3
  6.5 0.0 copy-start.2
  6.5 0.0 all-gather.3.cloned.1.call-start
  6.5 16.4 %attention.1 = bf16[32,1024]{1,0:T(8,128)(2,1)} custom-call(s32[128]{0:T(128)} %lengths.1, bf16[32,8,128]{2,1,0:T(8,128)(2,1)} %q_ref.1, bf16[32,1024,128]{2,1,0:T(8,128)(2,1)} %k_ref.1, bf16[32,1024,128]{2,1,0:T(8,128)(2,1)} %v_ref.1), custom_call_target="tpu_custom_call" | custom-call | tf_op jit(solution)/shard_map/attention/pallas_call | solution.py:53
  22.9 0.0 all-gather.3.cloned.1.call-update
  22.9 0.0 reduce-scatter.2.cloned.1.call-start
  23.0 0.0 copy-done.3
  23.0 40.7 %all-gather.3.cloned.1.call-done = bf16[512,1024]{1,0:T(8,128)(2,1)} async-done(((bf16[32,1024]{1,0:T(8,128)(2,1)}), bf16[512,1024]{1,0:T(8,128)(2,1)}) %all-gather.3.cloned.1.call-update) | async-done | bytes 1048592 | tf_op jit(solution)/shard_map/all_gather | solution.py:225
  63.7 0.0 copy-done
  63.7 0.0 copy-done.2
  63.7 1.8 multiply_reduce_fusion
  65.4 0.0 copy-start.1
  65.4 31.6 %psum.7 = f32[128]{0:T(128)S(1)} all-reduce(f32[128]{0:T(128)S(1)} %get-tuple-element.5), channel_id=1, replica_groups=mesh['groups'=2,'neuron'=16] {'neuron'}, use_global_device_ids=true, to_apply=%region_1.0 | all-reduce | flops 128 | bytes 1024 | tf_op jit(solution)/shard_map/psum | solution.py:231
  97.1 0.7 multiply_convert_fusion.x_ref
  97.8 11.8 %project_up.1 = f32[512,16,128]{2,1,0:T(8,128)} custom-call(s32[16,32]{1,0:T(8,128)} %picked.3, bf16[128,256]{1,0:T(8,128)(2,1)} %multiply_convert_fusion.x_ref, bf16[256,14336]{1,0:T(8,128)(2,1)} %gate_ref.1, bf16[256,14336]{1,0:T(8,128)(2,1)} %up_ref.1), custom_call_target="tpu_custom_call" | custom-call | tf_op jit(solution)/shard_map/project_up/pallas_call | solution.py:113
  109.6 0.0 copy-done.1
  109.6 0.0 reduce-scatter.2.cloned.1.call-update
  109.6 0.0 all-gather.5.cloned.1.call-start
  109.7 70.1 %reduce-scatter.2.cloned.1.call-done = f32[32,16,128]{2,1,0:T(8,128)} async-done(((f32[512,16,128]{2,1,0:T(8,128)}), f32[32,16,128]{2,1,0:T(8,128)}) %reduce-scatter.2.cloned.1.call-update) | async-done | bytes 262160 | tf_op jit(solution)/shard_map/reduce_scatter | solution.py:236
  179.7 1.6 fusion.1
  181.4 0.0 all-gather.5.cloned.1.call-update
  181.4 37.6 %all-gather.5.cloned.1.call-done.act_ref = bf16[256,16,128]{2,1,0:T(8,128)(2,1)} async-done(((bf16[16,16,128]{2,1,0:T(8,128)(2,1)}), bf16[256,16,128]{2,1,0:T(8,128)(2,1)}) %all-gather.5.cloned.1.call-update) | async-done | bytes 1048592 | tf_op jit(solution)/shard_map/all_gather | solution.py:239
  219.0 10.7 %project_down.1 = bf16[128,256]{1,0:T(8,128)(2,1)} custom-call(s32[16,32]{1,0:T(8,128)} %picked.3, bf16[256,16,128]{2,1,0:T(8,128)(2,1)} %all-gather.5.cloned.1.call-done.act_ref, bf16[14336,256]{1,0:T(8,128)(2,1)} %down_ref.1, f32[128,256]{1,0:T(8,128)} %copy-done.1), custom_call_target="tpu_custom_call" | custom-call | tf_op jit(solution)/shard_map/project_down/pallas_call | solution.py:179
  (2 shorter events, 0.0 us)
Async XLA Ops:
  6.5 57.1 %copy-start = (bf16[4096,256]{1,0:T(8,128)(2,1)S(1)}, bf16[4096,256]{1,0:T(8,128)(2,1)}, u32[]{:S(2)}) copy-start(bf16[4096,256]{1,0:T(8,128)(2,1)} %param.17) | copy-start | bytes 6291460
  6.5 16.4 %copy-start.3 = (bf16[256]{0:T(256)(128)(2,1)S(1)}, bf16[256]{0:T(256)(128)(2,1)}, u32[]{:S(2)}) copy-start(bf16[256]{0:T(256)(128)(2,1)} %param.18) | copy-start | bytes 1540
  6.5 57.1 %copy-start.2 = (bf16[128,256]{1,0:T(8,128)(2,1)S(1)}, bf16[128,256]{1,0:T(8,128)(2,1)}, u32[]{:S(2)}) copy-start(bf16[128,256]{1,0:T(8,128)(2,1)} %param.16) | copy-start | bytes 196612
  6.5 57.1 %all-gather.3.cloned.1.call-start = ((), (), s32[]{:S(2)}) async-start(), calls=%async_computation.1 | async-start | bytes 1114112 | tf_op jit(solution)/shard_map/all_gather | solution.py:225
  22.9 156.8 %reduce-scatter.2.cloned.1.call-start = ((), (), s32[]{:S(2)}) async-start(), calls=%async_computation.2 | async-start | bytes 4456448 | tf_op jit(solution)/shard_map/reduce_scatter | solution.py:236
  65.4 44.2 %copy-start.1 = (f32[128,256]{1,0:T(8,128)}, f32[128,256]{1,0:T(8,128)S(1)}, u32[]{:S(2)}) copy-start(f32[128,256]{1,0:T(8,128)S(1)} %get-tuple-element.6.stream_ref) | copy-start | bytes 393220
  109.6 109.3 %all-gather.5.cloned.1.call-start = ((), (), s32[]{:S(2)}) async-start(), calls=%async_computation.3 | async-start | bytes 1114112 | tf_op jit(solution)/shard_map/all_gather | solution.py:239
Sparse Core Ops, SparseCore 0:
  23.1 40.5 all-gather.2
  109.7 69.9 reduce-scatter.1
  181.9 36.9 all-gather.4

commit v2 on v1

--- a/solution.py
+++ b/solution.py
@@ -200,6 +200,271 @@
     )(picked, activated, down_weight, stream)
 
 
+MESH = pl.DeviceIdType.MESH
+
+
+def stage_count(members):
+    stages = members.bit_length() - 1
+    assert members == 1 << stages
+    return stages
+
+
+def bit_of(me, stage):
+    return lax.rem(me // (1 << stage), 2)
+
+
+def partner_of(me, stage):
+    return me + (1 << stage) * (1 - 2 * bit_of(me, stage))
+
+
+def place_of(me, stages):
+    place = 0
+    for stage in range(stages):
+        place = place + bit_of(me, stage) * (1 << (stages - 1 - stage))
+    return place
+
+
+def static_place(member, stages):
+    return sum(((member >> s) & 1) << (stages - 1 - s) for s in range(stages))
+
+
+def greet(peers):
+    barrier = pltpu.get_barrier_semaphore()
+    for peer in peers:
+        pl.semaphore_signal(barrier, inc=1, device_id={AXIS: peer}, device_id_type=MESH)
+    pl.semaphore_wait(barrier, len(peers))
+
+
+def send(src, dst, send_sem, recv_sem, peer):
+    return pltpu.make_async_remote_copy(
+        src_ref=src,
+        dst_ref=dst,
+        send_sem=send_sem,
+        recv_sem=recv_sem,
+        device_id={AXIS: peer},
+        device_id_type=MESH,
+    )
+
+
+def gather_kernel(
+    members, rows, att_ref, res_ref, gain_ref, w_hbm, stream_ref, normed_ref,
+    held, weight, sums, mine, send_sems, recv_sems, sum_send, sum_recv, own_sem, w_sem,
+):
+    stages = stage_count(members)
+    me = lax.axis_index(AXIS)
+    chunks, entries, span = held.shape[0], held.shape[2], held.shape[3]
+    w_copy = pltpu.make_async_copy(w_hbm, weight, w_sem)
+    w_copy.start()
+    place = place_of(me, stages)
+    own = [
+        pltpu.make_async_copy(
+            att_ref.at[:, c * span : (c + 1) * span], held.at[c, place], own_sem.at[c]
+        )
+        for c in range(chunks)
+    ]
+    for copy in own:
+        copy.start()
+    greet([lax.rem(me + step, members) for step in range(1, members)])
+    flying = {}
+
+    def start(c, k):
+        size = 1 << k
+        at = place // size * size
+        if k == 0:
+            src = att_ref.at[:, c * span : (c + 1) * span]
+            dst = held.at[c, place]
+        else:
+            src = held.at[c, pl.ds(at, size)]
+            dst = held.at[c, pl.ds(at, size)]
+        copy = send(
+            src, dst, send_sems.at[c, k], recv_sems.at[c, k], partner_of(me, stages - 1 - k)
+        )
+        copy.start()
+        flying[c, k] = copy
+
+    for c in range(chunks):
+        start(c, 0)
+    for copy in own:
+        copy.wait()
+    for c, k in sorted(
+        ((c, k) for c in range(chunks) for k in range(stages)), key=lambda ck: (ck[0] + ck[1], ck[0])
+    ):
+        flying[c, k].wait_recv()
+        if k + 1 < stages:
+            start(c, k + 1)
+    w_copy.wait()
+    total = res_ref[...].astype(jnp.float32)
+    per_head = rows // entries
+    for head in range(members // per_head):
+        for c in range(chunks):
+            lhs = jnp.concatenate(
+                [held[c, static_place(head * per_head + i, stages)] for i in range(per_head)], axis=0
+            )
+            first = (head * chunks + c) * span
+            total += jnp.dot(
+                lhs, weight[first : first + span, :], preferred_element_type=jnp.float32
+            )
+    stream_ref[...] = total
+    lane = sums.shape[2]
+    wide = jnp.broadcast_to(jnp.sum(total * total, axis=1, keepdims=True), (rows, lane))
+    mine[...] = jnp.transpose(wide)[: mine.shape[0], :]
+    copies = []
+    for step in range(1, members):
+        peer = lax.rem(me + step, members)
+        copy = send(mine, sums.at[step], sum_send.at[step], sum_recv.at[step], peer)
+        copy.start()
+        copies.append(copy)
+    row_sums = mine[...]
+    for step, copy in enumerate(copies, 1):
+        copy.wait_recv()
+        row_sums += sums[step]
+    spread = jnp.transpose(jnp.broadcast_to(row_sums[:1, :], (lane, rows)))
+    model = members * total.shape[1]
+    inverse = lax.rsqrt(spread[:, :1] / model + 1e-05)
+    normed_ref[...] = (total * inverse * gain_ref[...].astype(jnp.float32)).astype(normed_ref.dtype)
+    for copy in copies:
+        copy.wait_send()
+    for copy in flying.values():
+        copy.wait_send()
+
+
+def gather_and_norm(attended, residual, norm_gain, out_weight, members):
+    entries, mixed = attended.shape
+    rows, width = residual.shape
+    chunks = 2
+    stages = stage_count(members)
+    vmem = pl.BlockSpec(memory_space=pltpu.VMEM)
+    return pl.pallas_call(
+        functools.partial(gather_kernel, members, rows),
+        out_shape=(
+            jax.ShapeDtypeStruct((rows, width), jnp.float32),
+            jax.ShapeDtypeStruct((rows, width), jnp.bfloat16),
+        ),
+        in_specs=[vmem, vmem, vmem, pl.BlockSpec(memory_space=pl.ANY)],
+        out_specs=(vmem, vmem),
+        scratch_shapes=[
+            pltpu.VMEM((chunks, members, entries, mixed // chunks), jnp.bfloat16),
+            pltpu.VMEM(out_weight.shape, jnp.bfloat16),
+            pltpu.VMEM((members, 8, rows), jnp.float32),
+            pltpu.VMEM((8, rows), jnp.float32),
+            pltpu.SemaphoreType.DMA((chunks, stages)),
+            pltpu.SemaphoreType.DMA((chunks, stages)),
+            pltpu.SemaphoreType.DMA((members,)),
+            pltpu.SemaphoreType.DMA((members,)),
+            pltpu.SemaphoreType.DMA((chunks,)),
+            pltpu.SemaphoreType.DMA,
+        ],
+        compiler_params=pltpu.CompilerParams(
+            collective_id=0, has_side_effects=True, vmem_limit_bytes=VMEM_LIMIT
+        ),
+        name="gather_and_norm",
+    )(attended, residual, norm_gain.reshape(1, width), out_weight)
+
+
+def exchange_kernel(members, chunks, part_ref, act_ref, *scratch):
+    stages = stage_count(members)
+    me = lax.axis_index(AXIS)
+    recv = scratch[:stages]
+    out = (None,) + scratch[stages : 2 * stages - 1]
+    keep = scratch[2 * stages - 1 : 3 * stages - 2]
+    own, held, send_sems, recv_sems = scratch[3 * stages - 2 :]
+    size = part_ref.shape[0] // chunks
+    group_rows = part_ref.shape[1] // 2
+    piece = size // members
+    unit = piece // 2
+    place = place_of(me, stages)
+    greet([partner_of(me, stage) for stage in range(stages)])
+    flying = {}
+
+    def go(c, s, src, dst, stage):
+        copy = send(src, dst, send_sems.at[c, s], recv_sems.at[c, s], partner_of(me, stage))
+        copy.start()
+        flying[c, s] = copy
+
+    def start_gather(c, k):
+        count = 1 << k
+        at = pl.ds((place // count * count) * unit, count * unit)
+        src = own.at[c] if k == 0 else held.at[c, at]
+        go(c, stages + k, src, held.at[c, at], stages - 1 - k)
+
+    for c in range(chunks):
+        half = size // 2
+        away = c * size + (1 - bit_of(me, 0)) * half
+        go(c, 0, part_ref.at[pl.ds(away, half)], recv[0].at[c], 0)
+
+    def landed(c, s):
+        flying[c, s].wait_recv()
+        if s >= stages:
+            if s + 1 < 2 * stages:
+                start_gather(c, s + 1 - stages)
+            return
+        held_size = size >> (s + 1)
+
+        def added(at, count):
+            if s == 0:
+                base = c * size + bit_of(me, 0) * held_size
+                had = part_ref[pl.ds(base + at, count)].astype(jnp.float32)
+            else:
+                had = keep[s - 1][c, pl.ds(at, count)]
+            return had + recv[s][c, pl.ds(at, count)].astype(jnp.float32)
+
+        if s + 1 < stages:
+            half = held_size // 2
+            bit = bit_of(me, s + 1)
+            out[s + 1][c] = added((1 - bit) * half, half).astype(jnp.bfloat16)
+            go(c, s + 1, out[s + 1].at[c], recv[s + 1].at[c], s + 1)
+            keep[s][c] = added(bit * half, half)
+        else:
+            whole = added(0, held_size)
+            act = jnp.maximum(whole[:, :group_rows], 0.0) * whole[:, group_rows:]
+            act = act.reshape(unit, 2 * group_rows, act.shape[2]).astype(jnp.bfloat16)
+            own[c] = act
+            start_gather(c, 0)
+            held[c, pl.ds(place * unit, unit)] = act
+
+    for c, s in sorted(
+        ((c, s) for c in range(chunks) for s in range(2 * stages)),
+        key=lambda cs: (cs[1] > 0, cs[0] + cs[1], cs[0]),
+    ):
+        landed(c, s)
+    for c in range(chunks):
+        act_ref[pl.ds(c * size // 2, size // 2)] = held[c]
+    for copy in flying.values():
+        copy.wait_send()
+
+
+def exchange(parts, members):
+    pairs, height, blk = parts.shape
+    chunks = 4
+    stages = stage_count(members)
+    size = pairs // chunks
+    vmem = pl.BlockSpec(memory_space=pltpu.VMEM)
+    tile = (height, blk)
+
+    def buffers(kind, first, last):
+        return [pltpu.VMEM((chunks, size >> (s + 1)) + tile, kind) for s in range(first, last)]
+
+    return pl.pallas_call(
+        functools.partial(exchange_kernel, members, chunks),
+        out_shape=jax.ShapeDtypeStruct((pairs // 2,) + tile, jnp.bfloat16),
+        in_specs=[vmem],
+        out_specs=vmem,
+        scratch_shapes=buffers(jnp.bfloat16, 0, stages)
+        + buffers(jnp.bfloat16, 1, stages)
+        + buffers(jnp.float32, 1, stages)
+        + [
+            pltpu.VMEM((chunks, size // members // 2) + tile, jnp.bfloat16),
+            pltpu.VMEM((chunks, size // 2) + tile, jnp.bfloat16),
+            pltpu.SemaphoreType.DMA((chunks, 2 * stages)),
+            pltpu.SemaphoreType.DMA((chunks, 2 * stages)),
+        ],
+        compiler_params=pltpu.CompilerParams(
+            collective_id=1, has_side_effects=True, vmem_limit_bytes=VMEM_LIMIT
+        ),
+        name="exchange",
+    )(parts)
+
+
 BLK = 128
 
 
@@ -216,27 +481,11 @@
     up_weight,
     down_weight,
 ):
-    rows = residual.shape[0]
-    groups, active = active_blocks.shape
-    group_rows = rows // groups
     members = lax.axis_size(AXIS)
-    model = residual.shape[1] * members
     attended = attention(queries, keys, values, lengths)
-    gathered = lax.all_gather(attended, AXIS, axis=0, tiled=True)
-    by_head = gathered.reshape(gathered.shape[0] // rows, rows, gathered.shape[1])
-    out_heads = out_weight.reshape(by_head.shape[0], by_head.shape[2], out_weight.shape[1])
-    stream = residual.astype(jnp.float32) + jnp.einsum(
-        "hrc,hcd->rd", by_head, out_heads, preferred_element_type=jnp.float32
-    )
-    square_sums = lax.psum(jnp.sum(stream * stream, axis=1), AXIS)
-    normed = (
-        stream * lax.rsqrt(square_sums / model + 1e-05)[:, None] * norm_gain.astype(jnp.float32)
-    ).astype(jnp.bfloat16)
-    parts = project_up(normed, gate_weight, up_weight, active_blocks, BLK, jnp.float32)
-    mine = lax.psum_scatter(parts, AXIS, scatter_dimension=0, tiled=True)
-    act = (jnp.maximum(mine[:, :group_rows], 0.0) * mine[:, group_rows:]).astype(jnp.bfloat16)
-    act = act.reshape(act.shape[0] // 2, 2 * group_rows, act.shape[2])
-    activated = lax.all_gather(act, AXIS, axis=0, tiled=True)
+    stream, normed = gather_and_norm(attended, residual, norm_gain, out_weight, members)
+    parts = project_up(normed, gate_weight, up_weight, active_blocks, BLK, jnp.bfloat16)
+    activated = exchange(parts, members)
     return project_down(activated, down_weight, stream, active_blocks, BLK)
 
 

time: 237 us -> 110 us (0.46)
  waiting for transfers between devices: 148 us -> 0 us
  Pallas kernels: 38.9 us -> 108 us
  blocking collectives: 31.6 us -> 0 us
  between operations: 13.1 us -> 0.02 us
    all_gather x2 -> x0, waiting for transfers between devices: 78.2 us -> none  [the longest x1 40.7 us: body(): gathered = lax.all_gather(attended, AXIS, axis=0, tiled=True)]
    pallas_call x0 -> x2, Pallas kernels: none -> 70.3 us  [the longest x1 40.2 us: exchange(): pl.pallas_call(functools.partial(exchange_kernel, members, chunks), out_s...]
    reduce_scatter x1 -> x0, waiting for transfers between devices: 70.1 us -> none  [body(): mine = lax.psum_scatter(parts, AXIS, scatter_dimension=0, tiled=True)]
    psum x1 -> x0, blocking collectives: 31.6 us -> none  [body(): square_sums = lax.psum(jnp.sum(stream * stream, axis=1), AXIS)]
  transfers between devices with their start and end apart: 3 -> 0, of which waited for: 3 -> 0; matrix products, arithmetic and copies ran while one was open for 0% -> 0% of each run, Pallas kernels for 0% -> 0%
where the time goes in v2:
time: 110 us
  Pallas kernels  108 us (98%)
  local copies, waits for them, and re-layouts  1.22 us (1%)
    pallas_call x1, Pallas kernels, exchange(): pl.pallas_call(functools.partial(exchange_kernel, members, chunks), out_s...  40.2 us
    pallas_call x1, Pallas kernels, gather_and_norm(): pl.pallas_call(functools.partial(gather_kernel, members, rows), out_shape...  30.1 us
    pallas_call x1, Pallas kernels, attention(): pl.pallas_call(functools.partial(attention_kernel, per_step=per_step, row...  16.2 us
    pallas_call x1, Pallas kernels, project_up(): pl.pallas_call(up_kernel, out_shape=jax.ShapeDtypeStruct((groups * active...  11.2 us
    pallas_call x1, Pallas kernels, project_down(): pl.pallas_call(down_kernel, out_shape=jax.ShapeDtypeStruct((rows, width),...  10.7 us

profile of v2, /device:TPU:0, one launch (start us, length us, event | category | flops | bytes accessed | tf_op | source)
XLA Modules:
  0.0 109.6 jit_solution(1413776013372243196)
XLA Ops:
  0.0 1.2 %reshape.3.gain_ref = bf16[1,256]{1,0:T(2,128)(2,1)} reshape(bf16[256]{0:T(256)(128)(2,1)} %param.18) | data formatting | bytes 1024 | tf_op jit(solution)/shard_map/reshape | solution.py:361
  1.2 16.2 %attention.1.att_ref = bf16[32,1024]{1,0:T(8,128)(2,1)} custom-call(s32[128]{0:T(128)} %lengths.1, bf16[32,8,128]{2,1,0:T(8,128)(2,1)} %q_ref.1, bf16[32,1024,128]{2,1,0:T(8,128)(2,1)} %k_ref.1, bf16[32,1024,128]{2,1,0:T(8,128)(2,1)} %v_ref.1), custom_call_target="tpu_custom_call" | custom-call | tf_op jit(solution)/shard_map/attention/pallas_call | solution.py:53
  17.4 30.1 %gather_and_norm.1 = (f32[128,256]{1,0:T(8,128)}, bf16[128,256]{1,0:T(8,128)(2,1)}) custom-call(bf16[32,1024]{1,0:T(8,128)(2,1)} %attention.1.att_ref, bf16[128,256]{1,0:T(8,128)(2,1)} %res_ref.1, bf16[1,256]{1,0:T(2,128)(2,1)} %reshape.3.gain_ref, bf16[4096,256]{1,0:T(8,128)(2,1)} %w_hbm.1), custom_call_target="tpu_custom_call" | custom-call | tf_op jit(solution)/shard_map/gather_and_norm/pallas_call | solution.py:337
  47.5 11.2 %project_up.1.part_ref = bf16[512,16,128]{2,1,0:T(8,128)(2,1)} custom-call(s32[16,32]{1,0:T(8,128)} %picked.3, bf16[128,256]{1,0:T(8,128)(2,1)} %get-tuple-element.7.x_ref, bf16[256,14336]{1,0:T(8,128)(2,1)} %gate_ref.1, bf16[256,14336]{1,0:T(8,128)(2,1)} %up_ref.1), custom_call_target="tpu_custom_call" | custom-call | tf_op jit(solution)/shard_map/project_up/pallas_call | solution.py:113
  58.8 40.2 %exchange.1.act_ref = bf16[256,16,128]{2,1,0:T(8,128)(2,1)} custom-call(bf16[512,16,128]{2,1,0:T(8,128)(2,1)} %project_up.1.part_ref), custom_call_target="tpu_custom_call" | custom-call | tf_op jit(solution)/shard_map/exchange/pallas_call | solution.py:447
  98.9 10.7 %project_down.1 = bf16[128,256]{1,0:T(8,128)(2,1)} custom-call(s32[16,32]{1,0:T(8,128)} %picked.3, bf16[256,16,128]{2,1,0:T(8,128)(2,1)} %exchange.1.act_ref, bf16[14336,256]{1,0:T(8,128)(2,1)} %down_ref.1, f32[128,256]{1,0:T(8,128)} %get-tuple-element.8.stream_ref), custom_call_target="tpu_custom_call" | custom-call | tf_op jit(solution)/shard_map/project_down/pallas_call | solution.py:179

commit v3 on v2

--- a/solution.py
+++ b/solution.py
@@ -16,62 +16,6 @@
     while total % size:
         size -= 1
     return size
-
-
-def attention_kernel(lengths, q_ref, k_ref, v_ref, out_ref, held, few, *, per_step, rows):
-    step = pl.program_id(0)
-    entries, heads = out_ref.shape[0], q_ref.shape[1]
-    width, slots = q_ref.shape[2], k_ref.shape[1]
-    scale = width ** (-0.5)
-    first = lax.rem(lax.axis_index(AXIS) * entries, rows)
-    slot = lax.broadcasted_iota(jnp.int32, (heads, slots), 1)
-    for i in range(per_step):
-        e = step * per_step + i
-        live = slot < lengths[first + e]
-        scores = lax.dot_general(
-            q_ref[i], k_ref[i], (((1,), (1,)), ((), ())), preferred_element_type=jnp.float32
-        )
-        scores = jnp.where(live, scores * scale, -1e30)
-        top = jnp.max(scores, axis=1, keepdims=True)
-        weights = jnp.where(live, jnp.exp(scores - top), 0.0)
-        total = jnp.sum(weights, axis=1, keepdims=True)
-        probs = (weights * (1.0 / total)).astype(jnp.bfloat16)
-        mixed = jnp.dot(probs, v_ref[i], preferred_element_type=jnp.float32)
-        for j in range(heads):
-            few[i : i + 1, j * width : (j + 1) * width] = mixed[j : j + 1, :]
-    held[pl.ds(pl.multiple_of(step * per_step, per_step), per_step), :] = few[...]
-
-    @pl.when(step == pl.num_programs(0) - 1)
-    def _():
-        out_ref[...] = held[...].astype(out_ref.dtype)
-
-
-def attention(queries, keys, values, lengths):
-    entries, heads, width = queries.shape
-    slots = keys.shape[1]
-    per_step = fitting(entries, 8)
-    return pl.pallas_call(
-        functools.partial(attention_kernel, per_step=per_step, rows=lengths.shape[0]),
-        out_shape=jax.ShapeDtypeStruct((entries, heads * width), jnp.bfloat16),
-        grid_spec=pltpu.PrefetchScalarGridSpec(
-            num_scalar_prefetch=1,
-            grid=(entries // per_step,),
-            in_specs=[
-                pl.BlockSpec((per_step, heads, width), lambda s, n: (s, 0, 0)),
-                pl.BlockSpec((per_step, slots, width), lambda s, n: (s, 0, 0)),
-                pl.BlockSpec((per_step, slots, width), lambda s, n: (s, 0, 0)),
-            ],
-            out_specs=pl.BlockSpec((entries, heads * width), lambda s, n: (0, 0)),
-            scratch_shapes=[
-                pltpu.VMEM((entries, heads * width), jnp.float32),
-                pltpu.VMEM((per_step, heads * width), jnp.float32),
-            ],
-        ),
-        compiler_params=pltpu.CompilerParams(
-            dimension_semantics=("arbitrary",), vmem_limit_bytes=VMEM_LIMIT
-        ),
-        name="attention",
-    )(lengths, queries, keys, values)
 
 
 def up_kernel(picked, x_ref, gate_ref, up_ref, out_ref, gate_all, up_all):
@@ -133,71 +77,71 @@
     )(picked, normed, gate_weight, up_weight)
 
 
-def down_kernel(picked, act_ref, down_ref, stream_ref, out_ref, dense, total):
-    step = pl.program_id(0)
-    blk = dense.shape[2]
-    per_step = down_ref.shape[0] // blk
+def down_kernel(picked, act_ref, stream_ref, down_hbm, out_ref, dense, down, sems):
+    blocks, _, blk = dense.shape
+    parts = sems.shape[0]
     groups, active = picked.shape
     group_rows = dense.shape[1] // groups
-
-    @pl.when(step == 0)
-    def _():
-        @pl.loop(0, dense.shape[0])
-        def _(b):
-            dense[b] = jnp.zeros(dense.shape[1:], jnp.float32)
-
-        @pl.loop(0, groups)
-        def _(g):
-            row = pl.multiple_of(g * group_rows, group_rows)
-            for j in range(0, active, 2):
-                both = act_ref[(g * active + j) // 2].astype(jnp.float32)
-                dense[picked[g, j], pl.ds(row, group_rows), :] = both[:group_rows]
-                dense[picked[g, j + 1], pl.ds(row, group_rows), :] = both[group_rows:]
-
-        total[...] = stream_ref[...]
-
-    acc = total[...]
-    for pair in range(0, per_step, 2):
-        n = min(2, per_step - pair)
-        lhs = jnp.concatenate(
-            [dense[step * per_step + pair + i] for i in range(n)], axis=1
-        ).astype(jnp.bfloat16)
-        acc += jnp.dot(
-            lhs, down_ref[pair * blk : (pair + n) * blk, :], preferred_element_type=jnp.float32
+    size = down.shape[0] // parts
+    copies = [
+        pltpu.make_async_copy(
+            down_hbm.at[pl.ds(p * size, size)], down.at[pl.ds(p * size, size)], sems.at[p]
         )
-    total[...] = acc
-
-    @pl.when(step == pl.num_programs(0) - 1)
-    def _():
-        out_ref[...] = acc.astype(out_ref.dtype)
+        for p in range(parts)
+    ]
+    for copy in copies:
+        copy.start()
+
+    @pl.loop(0, blocks)
+    def _(b):
+        dense[b] = jnp.zeros(dense.shape[1:], jnp.float32)
+
+    @pl.loop(0, groups)
+    def _(g):
+        row = pl.multiple_of(g * group_rows, group_rows)
+        for j in range(0, active, 2):
+            both = act_ref[(g * active + j) // 2].astype(jnp.float32)
+            dense[picked[g, j], pl.ds(row, group_rows), :] = both[:group_rows]
+            dense[picked[g, j + 1], pl.ds(row, group_rows), :] = both[group_rows:]
+
+    acc = stream_ref[...]
+    per_part = blocks // parts
+    for p, copy in enumerate(copies):
+        copy.wait()
+        for pair in range(p * per_part, (p + 1) * per_part, 2):
+            n = min(2, (p + 1) * per_part - pair)
+            lhs = jnp.concatenate([dense[pair + i] for i in range(n)], axis=1)
+            acc += jnp.dot(
+                lhs.astype(jnp.bfloat16),
+                down[pair * blk : (pair + n) * blk, :],
+                preferred_element_type=jnp.float32,
+            )
+    out_ref[...] = acc.astype(out_ref.dtype)
 
 
 def project_down(activated, down_weight, stream, picked, blk):
     rows, width = stream.shape
     blocks = down_weight.shape[0] // blk
-    per_step = fitting(blocks, 16)
+    parts = blocks // fitting(blocks, 16)
+    vmem = pl.BlockSpec(memory_space=pltpu.VMEM)
     return pl.pallas_call(
         down_kernel,
         out_shape=jax.ShapeDtypeStruct((rows, width), jnp.bfloat16),
-        grid_spec=pltpu.PrefetchScalarGridSpec(
-            num_scalar_prefetch=1,
-            grid=(blocks // per_step,),
-            in_specs=[
-                pl.BlockSpec(activated.shape, lambda s, n: (0, 0, 0)),
-                pl.BlockSpec((per_step * blk, width), lambda s, n: (s, 0)),
-                pl.BlockSpec((rows, width), lambda s, n: (0, 0)),
-            ],
-            out_specs=pl.BlockSpec((rows, width), lambda s, n: (0, 0)),
-            scratch_shapes=[
-                pltpu.VMEM((blocks, rows, blk), jnp.float32),
-                pltpu.VMEM((rows, width), jnp.float32),
-            ],
-        ),
-        compiler_params=pltpu.CompilerParams(
-            dimension_semantics=("arbitrary",), vmem_limit_bytes=VMEM_LIMIT
-        ),
+        in_specs=[
+            pl.BlockSpec(memory_space=pltpu.SMEM),
+            vmem,
+            vmem,
+            pl.BlockSpec(memory_space=pl.ANY),
+        ],
+        out_specs=vmem,
+        scratch_shapes=[
+            pltpu.VMEM((blocks, rows, blk), jnp.float32),
+            pltpu.VMEM(down_weight.shape, jnp.bfloat16),
+            pltpu.SemaphoreType.DMA((parts,)),
+        ],
+        compiler_params=pltpu.CompilerParams(vmem_limit_bytes=VMEM_LIMIT),
         name="project_down",
-    )(picked, activated, down_weight, stream)
+    )(picked, activated, stream, down_weight)
 
 
 MESH = pl.DeviceIdType.MESH
@@ -246,64 +190,107 @@
     )
 
 
+def attend(q_ref, keys, values, few, lengths, first, begin):
+    heads, width = q_ref.shape[1:]
+    count, slots = keys.shape[:2]
+    slot = lax.broadcasted_iota(jnp.int32, (heads, slots), 1)
+    scores = []
+    for i in range(count):
+        part = lax.dot_general(
+            q_ref[begin + i], keys[i], (((1,), (1,)), ((), ())), preferred_element_type=jnp.float32
+        )
+        live = slot < lengths[first + begin + i]
+        scores.append(jnp.where(live, part * width ** (-0.5), -1e30))
+    scores = jnp.concatenate(scores, axis=0)
+    weights = jnp.exp(scores - jnp.max(scores, axis=1, keepdims=True))
+    probs = weights * (1.0 / jnp.sum(weights, axis=1, keepdims=True))
+    probs = probs.astype(jnp.bfloat16)
+    for i in range(count):
+        mixed = jnp.dot(
+            probs[i * heads : (i + 1) * heads], values[i], preferred_element_type=jnp.float32
+        )
+        for j in range(heads):
+            few[i : i + 1, j * width : (j + 1) * width] = mixed[j : j + 1, :]
+
+
 def gather_kernel(
-    members, rows, att_ref, res_ref, gain_ref, w_hbm, stream_ref, normed_ref,
-    held, weight, sums, mine, send_sems, recv_sems, sum_send, sum_recv, own_sem, w_sem,
+    members, rows, lengths, q_ref, res_ref, gain_ref, k_hbm, v_hbm, w_hbm, stream_ref, normed_ref,
+    keys, values, few, own, held, weight, sums, mine,
+    kv_sems, send_sems, recv_sems, sum_send, sum_recv, w_sem,
 ):
     stages = stage_count(members)
     me = lax.axis_index(AXIS)
-    chunks, entries, span = held.shape[0], held.shape[2], held.shape[3]
+    chunks, span = own.shape[0], own.shape[1]
+    entries, mixed = chunks * span, own.shape[2]
+    place = place_of(me, stages)
+    fetched = {}
+
+    def fetch(c):
+        for i, (hbm, slots) in enumerate(((k_hbm, keys), (v_hbm, values))):
+            copy = pltpu.make_async_copy(
+                hbm.at[pl.ds(c * span, span)], slots.at[c % 2], kv_sems.at[i, c % 2]
+            )
+            copy.start()
+            fetched[c, i] = copy
+
+    for c in range(min(2, chunks)):
+        fetch(c)
     w_copy = pltpu.make_async_copy(w_hbm, weight, w_sem)
-    w_copy.start()
-    place = place_of(me, stages)
-    own = [
-        pltpu.make_async_copy(
-            att_ref.at[:, c * span : (c + 1) * span], held.at[c, place], own_sem.at[c]
-        )
-        for c in range(chunks)
-    ]
-    for copy in own:
-        copy.start()
     greet([lax.rem(me + step, members) for step in range(1, members)])
     flying = {}
 
     def start(c, k):
         size = 1 << k
         at = place // size * size
-        if k == 0:
-            src = att_ref.at[:, c * span : (c + 1) * span]
-            dst = held.at[c, place]
-        else:
-            src = held.at[c, pl.ds(at, size)]
-            dst = held.at[c, pl.ds(at, size)]
+        src = own.at[c] if k == 0 else held.at[c, pl.ds(at, size)]
+        dst = held.at[c, place] if k == 0 else held.at[c, pl.ds(at, size)]
         copy = send(
             src, dst, send_sems.at[c, k], recv_sems.at[c, k], partner_of(me, stages - 1 - k)
         )
         copy.start()
         flying[c, k] = copy
 
-    for c in range(chunks):
-        start(c, 0)
-    for copy in own:
-        copy.wait()
-    for c, k in sorted(
-        ((c, k) for c in range(chunks) for k in range(stages)), key=lambda ck: (ck[0] + ck[1], ck[0])
-    ):
+    def landed(c, k):
         flying[c, k].wait_recv()
         if k + 1 < stages:
             start(c, k + 1)
+
+    first = lax.rem(me * entries, rows)
+    for c in range(chunks):
+        for i in range(2):
+            fetched[c, i].wait()
+        attend(q_ref, keys.at[c % 2], values.at[c % 2], few, lengths, first, c * span)
+        if c + 2 < chunks:
+            fetch(c + 2)
+        if c == 0:
+            w_copy.start()
+        block = few[...].astype(jnp.bfloat16)
+        own[c] = block
+        start(c, 0)
+        held[c, place] = block
+        for d in range(c):
+            if c - d - 1 < stages:
+                landed(d, c - d - 1)
+    for c, k in sorted(
+        ((c, k) for c in range(chunks) for k in range(max(0, chunks - 1 - c), stages)),
+        key=lambda ck: (ck[0] + ck[1], ck[0]),
+    ):
+        landed(c, k)
     w_copy.wait()
     total = res_ref[...].astype(jnp.float32)
     per_head = rows // entries
     for head in range(members // per_head):
-        for c in range(chunks):
-            lhs = jnp.concatenate(
-                [held[c, static_place(head * per_head + i, stages)] for i in range(per_head)], axis=0
-            )
-            first = (head * chunks + c) * span
-            total += jnp.dot(
-                lhs, weight[first : first + span, :], preferred_element_type=jnp.float32
-            )
+        lhs = jnp.concatenate(
+            [
+                held[c, static_place(head * per_head + i, stages)].astype(jnp.float32)
+                for i in range(per_head)
+                for c in range(chunks)
+            ],
+            axis=0,
+        ).astype(jnp.bfloat16)
+        total += jnp.dot(
+            lhs, weight[head * mixed : (head + 1) * mixed, :], preferred_element_type=jnp.float32
+        )
     stream_ref[...] = total
     lane = sums.shape[2]
     wide = jnp.broadcast_to(jnp.sum(total * total, axis=1, keepdims=True), (rows, lane))
@@ -328,37 +315,45 @@
         copy.wait_send()
 
 
-def gather_and_norm(attended, residual, norm_gain, out_weight, members):
-    entries, mixed = attended.shape
+def gather_and_norm(queries, keys, values, lengths, residual, norm_gain, out_weight, members):
+    entries, heads, head_width = queries.shape
+    slots = keys.shape[1]
     rows, width = residual.shape
-    chunks = 2
+    span = fitting(entries, 8)
+    chunks = entries // span
+    mixed = heads * head_width
     stages = stage_count(members)
     vmem = pl.BlockSpec(memory_space=pltpu.VMEM)
+    hbm = pl.BlockSpec(memory_space=pl.ANY)
     return pl.pallas_call(
         functools.partial(gather_kernel, members, rows),
         out_shape=(
             jax.ShapeDtypeStruct((rows, width), jnp.float32),
             jax.ShapeDtypeStruct((rows, width), jnp.bfloat16),
         ),
-        in_specs=[vmem, vmem, vmem, pl.BlockSpec(memory_space=pl.ANY)],
+        in_specs=[pl.BlockSpec(memory_space=pltpu.SMEM), vmem, vmem, vmem, hbm, hbm, hbm],
         out_specs=(vmem, vmem),
         scratch_shapes=[
-            pltpu.VMEM((chunks, members, entries, mixed // chunks), jnp.bfloat16),
+            pltpu.VMEM((2, span, slots, head_width), jnp.bfloat16),
+            pltpu.VMEM((2, span, slots, head_width), jnp.bfloat16),
+            pltpu.VMEM((span, mixed), jnp.float32),
+            pltpu.VMEM((chunks, span, mixed), jnp.bfloat16),
+            pltpu.VMEM((chunks, members, span, mixed), jnp.bfloat16),
             pltpu.VMEM(out_weight.shape, jnp.bfloat16),
             pltpu.VMEM((members, 8, rows), jnp.float32),
             pltpu.VMEM((8, rows), jnp.float32),
+            pltpu.SemaphoreType.DMA((2, 2)),
             pltpu.SemaphoreType.DMA((chunks, stages)),
             pltpu.SemaphoreType.DMA((chunks, stages)),
             pltpu.SemaphoreType.DMA((members,)),
             pltpu.SemaphoreType.DMA((members,)),
-            pltpu.SemaphoreType.DMA((chunks,)),
             pltpu.SemaphoreType.DMA,
         ],
         compiler_params=pltpu.CompilerParams(
             collective_id=0, has_side_effects=True, vmem_limit_bytes=VMEM_LIMIT
         ),
         name="gather_and_norm",
-    )(attended, residual, norm_gain.reshape(1, width), out_weight)
+    )(lengths, queries, residual, norm_gain.reshape(1, width), keys, values, out_weight)
 
 
 def exchange_kernel(members, chunks, part_ref, act_ref, *scratch):
@@ -482,8 +477,9 @@
     down_weight,
 ):
     members = lax.axis_size(AXIS)
-    attended = attention(queries, keys, values, lengths)
-    stream, normed = gather_and_norm(attended, residual, norm_gain, out_weight, members)
+    stream, normed = gather_and_norm(
+        queries, keys, values, lengths, residual, norm_gain, out_weight, members
+    )
     parts = project_up(normed, gate_weight, up_weight, active_blocks, BLK, jnp.bfloat16)
     activated = exchange(parts, members)
     return project_down(activated, down_weight, stream, active_blocks, BLK)

time: 110 us -> 95.1 us (0.86)
  Pallas kernels: 108 us -> 93.5 us
    pallas_call x1 -> x0, Pallas kernels: 16.2 us -> none  [attention(): pl.pallas_call(functools.partial(attention_kernel, per_step=per_step, row...]
    pallas_call x1, Pallas kernels: 30.1 us -> 34.6 us  [gather_and_norm(): pl.pallas_call(functools.partial(gather_kernel, members, rows), out_shape...]
    pallas_call x1, Pallas kernels: 10.7 us -> 6.85 us  [project_down(): pl.pallas_call(down_kernel, out_shape=jax.ShapeDtypeStruct((rows, width),...]
where the time goes in v3:
time: 95.1 us; the launch traced here: 94.7 us
  Pallas kernels  93.5 us (98%)
  local copies, waits for them, and re-layouts  1.22 us (1%)
    pallas_call x1, Pallas kernels, exchange(): pl.pallas_call(functools.partial(exchange_kernel, members, chunks), out_s...  40.8 us
    pallas_call x1, Pallas kernels, gather_and_norm(): pl.pallas_call(functools.partial(gather_kernel, members, rows), out_shape...  34.6 us
    pallas_call x1, Pallas kernels, project_up(): pl.pallas_call(up_kernel, out_shape=jax.ShapeDtypeStruct((groups * active...  11.2 us
    pallas_call x1, Pallas kernels, project_down(): pl.pallas_call(down_kernel, out_shape=jax.ShapeDtypeStruct((rows, width),...  6.85 us

profile of v3, /device:TPU:0, one launch (start us, length us, event | category | flops | bytes accessed | tf_op | source)
XLA Modules:
  0.0 94.7 jit_solution(8521969649631817745)
XLA Ops:
  0.0 1.2 %reshape.3.gain_ref = bf16[1,256]{1,0:T(2,128)(2,1)} reshape(bf16[256]{0:T(256)(128)(2,1)} %param.18) | data formatting | bytes 1024 | tf_op jit(solution)/shard_map/reshape | solution.py:356
  1.2 34.6 %gather_and_norm.1 = (f32[128,256]{1,0:T(8,128)}, bf16[128,256]{1,0:T(8,128)(2,1)}) custom-call(s32[128]{0:T(128)} %lengths.1, bf16[32,8,128]{2,1,0:T(8,128)(2,1)} %q_ref.1, bf16[128,256]{1,0:T(8,128)(2,1)} %res_ref.1, bf16[1,256]{1,0:T(2,128)(2,1)} %reshape.3.gain_ref, bf16[32,1024,128]{2,1,0:T(8,128)(2,1)} %k_hbm.1, bf16[32,1024,128]{2,1,0:T(8,128)(2,1)} %v_hbm.1, ...), custom_call_target="tpu_custom_call" | custom-call | tf_op jit(solution)/shard_map/gather_and_norm/pallas_call | solution.py:328
  35.8 11.2 %project_up.1.part_ref = bf16[512,16,128]{2,1,0:T(8,128)(2,1)} custom-call(s32[16,32]{1,0:T(8,128)} %picked.3, bf16[128,256]{1,0:T(8,128)(2,1)} %get-tuple-element.7.x_ref, bf16[256,14336]{1,0:T(8,128)(2,1)} %gate_ref.1, bf16[256,14336]{1,0:T(8,128)(2,1)} %up_ref.1), custom_call_target="tpu_custom_call" | custom-call | tf_op jit(solution)/shard_map/project_up/pallas_call | solution.py:57
  47.1 40.8 %exchange.1.act_ref = bf16[256,16,128]{2,1,0:T(8,128)(2,1)} custom-call(bf16[512,16,128]{2,1,0:T(8,128)(2,1)} %project_up.1.part_ref), custom_call_target="tpu_custom_call" | custom-call | tf_op jit(solution)/shard_map/exchange/pallas_call | solution.py:442
  87.9 6.8 %project_down.1 = bf16[128,256]{1,0:T(8,128)(2,1)} custom-call(s32[16,32]{1,0:T(8,128)} %picked.3, bf16[256,16,128]{2,1,0:T(8,128)(2,1)} %exchange.1.act_ref, f32[128,256]{1,0:T(8,128)} %get-tuple-element.8.stream_ref, bf16[14336,256]{1,0:T(8,128)(2,1)} %down_hbm.1), custom_call_target="tpu_custom_call" | custom-call | tf_op jit(solution)/shard_map/project_down/pallas_call | solution.py:127

commit v4 on v3

--- a/solution.py
+++ b/solution.py
@@ -16,65 +16,6 @@
     while total % size:
         size -= 1
     return size
-
-
-def up_kernel(picked, x_ref, gate_ref, up_ref, out_ref, gate_all, up_all):
-    step = pl.program_id(0)
-    blk = gate_all.shape[2]
-    per_step = gate_ref.shape[1] // blk
-    groups, active = picked.shape
-    group_rows = x_ref.shape[0] // groups
-    x = x_ref[...]
-    for pair in range(0, per_step, 2):
-        n = min(2, per_step - pair)
-        cols = slice(pair * blk, (pair + n) * blk)
-        for w_ref, dense in ((gate_ref, gate_all), (up_ref, up_all)):
-            part = jnp.dot(x, w_ref[:, cols], preferred_element_type=jnp.float32)
-            for i in range(n):
-                dense[step * per_step + pair + i] = part[:, i * blk : (i + 1) * blk]
-
-    @pl.when(step == pl.num_programs(0) - 1)
-    def _():
-        @pl.loop(0, groups)
-        def _(g):
-            row = pl.multiple_of(g * group_rows, group_rows)
-            for j in range(active):
-                b = picked[g, j]
-                both = jnp.concatenate(
-                    [gate_all[b, pl.ds(row, group_rows), :], up_all[b, pl.ds(row, group_rows), :]],
-                    axis=0,
-                )
-                out_ref[g * active + j] = both.astype(out_ref.dtype)
-
-
-def project_up(normed, gate_weight, up_weight, picked, blk, out_type):
-    rows, width = normed.shape
-    ff = gate_weight.shape[1]
-    blocks = ff // blk
-    groups, active = picked.shape
-    group_rows = rows // groups
-    per_step = fitting(blocks, 16)
-    return pl.pallas_call(
-        up_kernel,
-        out_shape=jax.ShapeDtypeStruct((groups * active, 2 * group_rows, blk), out_type),
-        grid_spec=pltpu.PrefetchScalarGridSpec(
-            num_scalar_prefetch=1,
-            grid=(blocks // per_step,),
-            in_specs=[
-                pl.BlockSpec((rows, width), lambda s, n: (0, 0)),
-                pl.BlockSpec((width, per_step * blk), lambda s, n: (0, s)),
-                pl.BlockSpec((width, per_step * blk), lambda s, n: (0, s)),
-            ],
-            out_specs=pl.BlockSpec(
-                (groups * active, 2 * group_rows, blk), lambda s, n: (0, 0, 0)
-            ),
-            scratch_shapes=[pltpu.VMEM((blocks, rows, blk), jnp.float32)] * 2,
-        ),
-        compiler_params=pltpu.CompilerParams(
-            dimension_semantics=("arbitrary",), vmem_limit_bytes=VMEM_LIMIT
-        ),
-        name="project_up",
-    )(picked, normed, gate_weight, up_weight)
 
 
 def down_kernel(picked, act_ref, stream_ref, down_hbm, out_ref, dense, down, sems):
@@ -213,10 +154,11 @@
             few[i : i + 1, j * width : (j + 1) * width] = mixed[j : j + 1, :]
 
 
-def gather_kernel(
-    members, rows, lengths, q_ref, res_ref, gain_ref, k_hbm, v_hbm, w_hbm, stream_ref, normed_ref,
-    keys, values, few, own, held, weight, sums, mine,
+def layer_kernel(
+    members, rows, lengths, picked, q_ref, res_ref, gain_ref, k_hbm, v_hbm, w_hbm, gate_hbm, up_hbm,
+    stream_ref, act_ref, keys, values, few, own, held, weight, sums, mine,
     kv_sems, send_sems, recv_sems, sum_send, sum_recv, w_sem,
+    gate, up, gate_all, up_all, part_ref, wide_sems, *exchange_scratch,
 ):
     stages = stage_count(members)
     me = lax.axis_index(AXIS)
@@ -236,6 +178,8 @@
     for c in range(min(2, chunks)):
         fetch(c)
     w_copy = pltpu.make_async_copy(w_hbm, weight, w_sem)
+    gate_copy = pltpu.make_async_copy(gate_hbm, gate, wide_sems.at[0])
+    up_copy = pltpu.make_async_copy(up_hbm, up, wide_sems.at[1])
     greet([lax.rem(me + step, members) for step in range(1, members)])
     flying = {}
 
@@ -264,6 +208,9 @@
             fetch(c + 2)
         if c == 0:
             w_copy.start()
+        if c == min(1, chunks - 1):
+            gate_copy.start()
+            up_copy.start()
         block = few[...].astype(jnp.bfloat16)
         own[c] = block
         start(c, 0)
@@ -308,14 +255,128 @@
     spread = jnp.transpose(jnp.broadcast_to(row_sums[:1, :], (lane, rows)))
     model = members * total.shape[1]
     inverse = lax.rsqrt(spread[:, :1] / model + 1e-05)
-    normed_ref[...] = (total * inverse * gain_ref[...].astype(jnp.float32)).astype(normed_ref.dtype)
+    gain = gain_ref[...].astype(jnp.float32)
+    normed = (total * inverse * gain).astype(jnp.bfloat16)
+    gate_copy.wait()
+    up_copy.wait()
+    project_up(normed, gate, up, gate_all, up_all)
+    exchange(members, picked, gate_all, up_all, part_ref, act_ref, *exchange_scratch)
     for copy in copies:
         copy.wait_send()
     for copy in flying.values():
         copy.wait_send()
 
 
-def gather_and_norm(queries, keys, values, lengths, residual, norm_gain, out_weight, members):
+def project_up(normed, gate, up, gate_all, up_all):
+    blocks, _, blk = gate_all.shape
+    per_dot = fitting(blocks, 2)
+    per_step = fitting(blocks // per_dot, 4)
+    span = per_dot * blk
+
+    @pl.loop(0, blocks // (per_dot * per_step))
+    def _(step):
+        for i in range(per_step):
+            dot = step * per_step + i
+            cols = pl.ds(pl.multiple_of(dot * span, span), span)
+            for weight, dense in ((gate, gate_all), (up, up_all)):
+                part = jnp.dot(normed, weight[:, cols], preferred_element_type=jnp.float32)
+                for n in range(per_dot):
+                    dense[dot * per_dot + n] = part[:, n * blk : (n + 1) * blk]
+
+
+def exchange(members, picked, gate_all, up_all, part_ref, act_ref, *scratch):
+    stages = stage_count(members)
+    me = lax.axis_index(AXIS)
+    recv = scratch[:stages]
+    out = (None,) + scratch[stages : 2 * stages - 1]
+    keep = scratch[2 * stages - 1 : 3 * stages - 2]
+    own, held, send_sems, recv_sems = scratch[3 * stages - 2 :]
+    chunks = held.shape[0]
+    groups, active = picked.shape
+    chunk_groups = groups // chunks
+    size = part_ref.shape[0] // chunks
+    group_rows = part_ref.shape[1] // 2
+    piece = size // members
+    unit = piece // 2
+    place = place_of(me, stages)
+    flying = {}
+
+    def go(c, s, src, dst, stage):
+        copy = send(src, dst, send_sems.at[c, s], recv_sems.at[c, s], partner_of(me, stage))
+        copy.start()
+        flying[c, s] = copy
+
+    def start_gather(c, k):
+        count = 1 << k
+        at = pl.ds((place // count * count) * unit, count * unit)
+        src = own.at[c] if k == 0 else held.at[c, at]
+        go(c, stages + k, src, held.at[c, at], stages - 1 - k)
+
+    def pick(c):
+        @pl.loop(c * chunk_groups, (c + 1) * chunk_groups)
+        def _(g):
+            row = pl.multiple_of(g * group_rows, group_rows)
+            for j in range(active):
+                b = picked[g, j]
+                both = jnp.concatenate(
+                    [gate_all[b, pl.ds(row, group_rows), :], up_all[b, pl.ds(row, group_rows), :]],
+                    axis=0,
+                )
+                part_ref[g * active + j] = both.astype(part_ref.dtype)
+
+    def start_scatter(c):
+        half = size // 2
+        away = c * size + (1 - bit_of(me, 0)) * half
+        go(c, 0, part_ref.at[pl.ds(away, half)], recv[0].at[c], 0)
+
+    def landed(c, s):
+        flying[c, s].wait_recv()
+        if s >= stages:
+            if s + 1 < 2 * stages:
+                start_gather(c, s + 1 - stages)
+            return
+        held_size = size >> (s + 1)
+
+        def added(at, count):
+            if s == 0:
+                base = c * size + bit_of(me, 0) * held_size
+                had = part_ref[pl.ds(base + at, count)].astype(jnp.float32)
+            else:
+                had = keep[s - 1][c, pl.ds(at, count)]
+            return had + recv[s][c, pl.ds(at, count)].astype(jnp.float32)
+
+        if s + 1 < stages:
+            half = held_size // 2
+            bit = bit_of(me, s + 1)
+            out[s + 1][c] = added((1 - bit) * half, half).astype(jnp.bfloat16)
+            go(c, s + 1, out[s + 1].at[c], recv[s + 1].at[c], s + 1)
+            keep[s][c] = added(bit * half, half)
+        else:
+            whole = added(0, held_size)
+            act = jnp.maximum(whole[:, :group_rows], 0.0) * whole[:, group_rows:]
+            act = act.reshape(unit, 2 * group_rows, act.shape[2]).astype(jnp.bfloat16)
+            own[c] = act
+            start_gather(c, 0)
+            held[c, pl.ds(place * unit, unit)] = act
+
+    for c in range(chunks):
+        pick(c)
+        start_scatter(c)
+    for c, s in sorted(
+        ((c, s) for c in range(chunks) for s in range(2 * stages)),
+        key=lambda cs: (cs[0] + cs[1], cs[0]),
+    ):
+        landed(c, s)
+    for c in range(chunks):
+        act_ref[pl.ds(c * size // 2, size // 2)] = held[c]
+    for copy in flying.values():
+        copy.wait_send()
+
+
+def until_activated(
+    queries, keys, values, lengths, picked, residual, norm_gain, out_weight, gate_weight, up_weight,
+    members, blk,
+):
     entries, heads, head_width = queries.shape
     slots = keys.shape[1]
     rows, width = residual.shape
@@ -323,15 +384,26 @@
     chunks = entries // span
     mixed = heads * head_width
     stages = stage_count(members)
+    blocks = gate_weight.shape[1] // blk
+    groups, active = picked.shape
+    pairs = groups * active
+    tile = (2 * rows // groups, blk)
+    parts = min(8, groups, pairs // (2 * members))
+    size = pairs // parts
+
+    def buffers(kind, begin, end):
+        return [pltpu.VMEM((parts, size >> (s + 1)) + tile, kind) for s in range(begin, end)]
+
     vmem = pl.BlockSpec(memory_space=pltpu.VMEM)
+    smem = pl.BlockSpec(memory_space=pltpu.SMEM)
     hbm = pl.BlockSpec(memory_space=pl.ANY)
     return pl.pallas_call(
-        functools.partial(gather_kernel, members, rows),
+        functools.partial(layer_kernel, members, rows),
         out_shape=(
             jax.ShapeDtypeStruct((rows, width), jnp.float32),
-            jax.ShapeDtypeStruct((rows, width), jnp.bfloat16),
+            jax.ShapeDtypeStruct((pairs // 2,) + tile, jnp.bfloat16),
         ),
-        in_specs=[pl.BlockSpec(memory_space=pltpu.SMEM), vmem, vmem, vmem, hbm, hbm, hbm],
+        in_specs=[smem, smem, vmem, vmem, vmem, hbm, hbm, hbm, hbm, hbm],
         out_specs=(vmem, vmem),
         scratch_shapes=[
             pltpu.VMEM((2, span, slots, head_width), jnp.bfloat16),
@@ -348,116 +420,30 @@
             pltpu.SemaphoreType.DMA((members,)),
             pltpu.SemaphoreType.DMA((members,)),
             pltpu.SemaphoreType.DMA,
+            pltpu.VMEM(gate_weight.shape, jnp.bfloat16),
+            pltpu.VMEM(up_weight.shape, jnp.bfloat16),
+            pltpu.VMEM((blocks, rows, blk), jnp.float32),
+            pltpu.VMEM((blocks, rows, blk), jnp.float32),
+            pltpu.VMEM((pairs,) + tile, jnp.bfloat16),
+            pltpu.SemaphoreType.DMA((2,)),
+        ]
+        + buffers(jnp.bfloat16, 0, stages)
+        + buffers(jnp.bfloat16, 1, stages)
+        + buffers(jnp.float32, 1, stages)
+        + [
+            pltpu.VMEM((parts, size // members // 2) + tile, jnp.bfloat16),
+            pltpu.VMEM((parts, size // 2) + tile, jnp.bfloat16),
+            pltpu.SemaphoreType.DMA((parts, 2 * stages)),
+            pltpu.SemaphoreType.DMA((parts, 2 * stages)),
         ],
         compiler_params=pltpu.CompilerParams(
             collective_id=0, has_side_effects=True, vmem_limit_bytes=VMEM_LIMIT
         ),
-        name="gather_and_norm",
-    )(lengths, queries, residual, norm_gain.reshape(1, width), keys, values, out_weight)
-
-
-def exchange_kernel(members, chunks, part_ref, act_ref, *scratch):
-    stages = stage_count(members)
-    me = lax.axis_index(AXIS)
-    recv = scratch[:stages]
-    out = (None,) + scratch[stages : 2 * stages - 1]
-    keep = scratch[2 * stages - 1 : 3 * stages - 2]
-    own, held, send_sems, recv_sems = scratch[3 * stages - 2 :]
-    size = part_ref.shape[0] // chunks
-    group_rows = part_ref.shape[1] // 2
-    piece = size // members
-    unit = piece // 2
-    place = place_of(me, stages)
-    greet([partner_of(me, stage) for stage in range(stages)])
-    flying = {}
-
-    def go(c, s, src, dst, stage):
-        copy = send(src, dst, send_sems.at[c, s], recv_sems.at[c, s], partner_of(me, stage))
-        copy.start()
-        flying[c, s] = copy
-
-    def start_gather(c, k):
-        count = 1 << k
-        at = pl.ds((place // count * count) * unit, count * unit)
-        src = own.at[c] if k == 0 else held.at[c, at]
-        go(c, stages + k, src, held.at[c, at], stages - 1 - k)
-
-    for c in range(chunks):
-        half = size // 2
-        away = c * size + (1 - bit_of(me, 0)) * half
-        go(c, 0, part_ref.at[pl.ds(away, half)], recv[0].at[c], 0)
-
-    def landed(c, s):
-        flying[c, s].wait_recv()
-        if s >= stages:
-            if s + 1 < 2 * stages:
-                start_gather(c, s + 1 - stages)
-            return
-        held_size = size >> (s + 1)
-
-        def added(at, count):
-            if s == 0:
-                base = c * size + bit_of(me, 0) * held_size
-                had = part_ref[pl.ds(base + at, count)].astype(jnp.float32)
-            else:
-                had = keep[s - 1][c, pl.ds(at, count)]
-            return had + recv[s][c, pl.ds(at, count)].astype(jnp.float32)
-
-        if s + 1 < stages:
-            half = held_size // 2
-            bit = bit_of(me, s + 1)
-            out[s + 1][c] = added((1 - bit) * half, half).astype(jnp.bfloat16)
-            go(c, s + 1, out[s + 1].at[c], recv[s + 1].at[c], s + 1)
-            keep[s][c] = added(bit * half, half)
-        else:
-            whole = added(0, held_size)
-            act = jnp.maximum(whole[:, :group_rows], 0.0) * whole[:, group_rows:]
-            act = act.reshape(unit, 2 * group_rows, act.shape[2]).astype(jnp.bfloat16)
-            own[c] = act
-            start_gather(c, 0)
-            held[c, pl.ds(place * unit, unit)] = act
-
-    for c, s in sorted(
-        ((c, s) for c in range(chunks) for s in range(2 * stages)),
-        key=lambda cs: (cs[1] > 0, cs[0] + cs[1], cs[0]),
-    ):
-        landed(c, s)
-    for c in range(chunks):
-        act_ref[pl.ds(c * size // 2, size // 2)] = held[c]
-    for copy in flying.values():
-        copy.wait_send()
-
-
-def exchange(parts, members):
-    pairs, height, blk = parts.shape
-    chunks = 4
-    stages = stage_count(members)
-    size = pairs // chunks
-    vmem = pl.BlockSpec(memory_space=pltpu.VMEM)
-    tile = (height, blk)
-
-    def buffers(kind, first, last):
-        return [pltpu.VMEM((chunks, size >> (s + 1)) + tile, kind) for s in range(first, last)]
-
-    return pl.pallas_call(
-        functools.partial(exchange_kernel, members, chunks),
-        out_shape=jax.ShapeDtypeStruct((pairs // 2,) + tile, jnp.bfloat16),
-        in_specs=[vmem],
-        out_specs=vmem,
-        scratch_shapes=buffers(jnp.bfloat16, 0, stages)
-        + buffers(jnp.bfloat16, 1, stages)
-        + buffers(jnp.float32, 1, stages)
-        + [
-            pltpu.VMEM((chunks, size // members // 2) + tile, jnp.bfloat16),
-            pltpu.VMEM((chunks, size // 2) + tile, jnp.bfloat16),
-            pltpu.SemaphoreType.DMA((chunks, 2 * stages)),
-            pltpu.SemaphoreType.DMA((chunks, 2 * stages)),
-        ],
-        compiler_params=pltpu.CompilerParams(
-            collective_id=1, has_side_effects=True, vmem_limit_bytes=VMEM_LIMIT
-        ),
-        name="exchange",
-    )(parts)
+        name="until_activated",
+    )(
+        lengths, picked, queries, residual, norm_gain.reshape(1, width),
+        keys, values, out_weight, gate_weight, up_weight,
+    )
 
 
 BLK = 128
@@ -477,11 +463,10 @@
     down_weight,
 ):
     members = lax.axis_size(AXIS)
-    stream, normed = gather_and_norm(
-        queries, keys, values, lengths, residual, norm_gain, out_weight, members
+    stream, activated = until_activated(
+        queries, keys, values, lengths, active_blocks, residual, norm_gain, out_weight,
+        gate_weight, up_weight, members, BLK,
     )
-    parts = project_up(normed, gate_weight, up_weight, active_blocks, BLK, jnp.bfloat16)
-    activated = exchange(parts, members)
     return project_down(activated, down_weight, stream, active_blocks, BLK)
 
 

time: 95.1 us -> 93.2 us (0.980)
  Pallas kernels: 93.5 us -> 91.8 us
    pallas_call x3 -> x1, Pallas kernels: 86.6 us -> 84.9 us  [until_activated(): pl.pallas_call(functools.partial(layer_kernel, members, rows), out_shape=...]
where the time goes in v4:
time: 93.2 us; the launch traced here: 93 us
  Pallas kernels  91.8 us (98%)
  local copies, waits for them, and re-layouts  1.22 us (1%)
    pallas_call x1, Pallas kernels, until_activated(): pl.pallas_call(functools.partial(layer_kernel, members, rows), out_shape=...  84.9 us
    pallas_call x1, Pallas kernels, project_down(): pl.pallas_call(down_kernel, out_shape=jax.ShapeDtypeStruct((rows, width),...  6.85 us

profile of v4, /device:TPU:0, one launch (start us, length us, event | category | flops | bytes accessed | tf_op | source)
XLA Modules:
  0.0 93.0 jit_solution(5051842279507017052)
XLA Ops:
  0.0 1.2 %reshape.3.gain_ref = bf16[1,256]{1,0:T(2,128)(2,1)} reshape(bf16[256]{0:T(256)(128)(2,1)} %param.18) | data formatting | bytes 1024 | tf_op jit(solution)/shard_map/reshape | solution.py:444
  1.2 84.9 %until_activated.1 = (f32[128,256]{1,0:T(8,128)}, bf16[256,16,128]{2,1,0:T(8,128)(2,1)}) custom-call(s32[128]{0:T(128)} %lengths.1, s32[16,32]{1,0:T(8,128)} %picked.3, bf16[32,8,128]{2,1,0:T(8,128)(2,1)} %q_ref.1, bf16[128,256]{1,0:T(8,128)(2,1)} %res_ref.1, bf16[1,256]{1,0:T(2,128)(2,1)} %reshape.3.gain_ref, bf16[32,1024,128]{2,1,0:T(8,128)(2,1)} %k_hbm.1, ...), custom_call_target="tpu_custom_call" | custom-call | tf_op jit(solution)/shard_map/until_activated/pallas_call | solution.py:400
  86.1 6.9 %project_down.1 = bf16[128,256]{1,0:T(8,128)(2,1)} custom-call(s32[16,32]{1,0:T(8,128)} %picked.3, bf16[256,16,128]{2,1,0:T(8,128)(2,1)} %get-tuple-element.7.act_ref, f32[128,256]{1,0:T(8,128)} %get-tuple-element.8.stream_ref, bf16[14336,256]{1,0:T(8,128)(2,1)} %down_hbm.1), custom_call_target="tpu_custom_call" | custom-call | tf_op jit(solution)/shard_map/project_down/pallas_call | solution.py:68

commit v5 on v4

--- a/solution.py
+++ b/solution.py
@@ -158,7 +158,7 @@
     members, rows, lengths, picked, q_ref, res_ref, gain_ref, k_hbm, v_hbm, w_hbm, gate_hbm, up_hbm,
     stream_ref, act_ref, keys, values, few, own, held, weight, sums, mine,
     kv_sems, send_sems, recv_sems, sum_send, sum_recv, w_sem,
-    gate, up, gate_all, up_all, part_ref, wide_sems, *exchange_scratch,
+    gate, up, gate_all, up_all, part_ref, inverse, wide_sems, *exchange_scratch,
 ):
     stages = stage_count(members)
     me = lax.axis_index(AXIS)
@@ -248,19 +248,18 @@
         copy = send(mine, sums.at[step], sum_send.at[step], sum_recv.at[step], peer)
         copy.start()
         copies.append(copy)
+    scaled = (total * gain_ref[...].reshape(1, total.shape[1]).astype(jnp.float32)).astype(jnp.bfloat16)
+    gate_copy.wait()
+    up_copy.wait()
+    project_up(scaled, gate, up, gate_all, up_all)
     row_sums = mine[...]
     for step, copy in enumerate(copies, 1):
         copy.wait_recv()
         row_sums += sums[step]
-    spread = jnp.transpose(jnp.broadcast_to(row_sums[:1, :], (lane, rows)))
+    spread = jnp.transpose(jnp.broadcast_to(row_sums[:1, :], (inverse.shape[1], rows)))
     model = members * total.shape[1]
-    inverse = lax.rsqrt(spread[:, :1] / model + 1e-05)
-    gain = gain_ref[...].astype(jnp.float32)
-    normed = (total * inverse * gain).astype(jnp.bfloat16)
-    gate_copy.wait()
-    up_copy.wait()
-    project_up(normed, gate, up, gate_all, up_all)
-    exchange(members, picked, gate_all, up_all, part_ref, act_ref, *exchange_scratch)
+    inverse[...] = lax.rsqrt(spread / model + 1e-05)
+    exchange(members, picked, inverse, gate_all, up_all, part_ref, act_ref, *exchange_scratch)
     for copy in copies:
         copy.wait_send()
     for copy in flying.values():
@@ -284,7 +283,7 @@
                     dense[dot * per_dot + n] = part[:, n * blk : (n + 1) * blk]
 
 
-def exchange(members, picked, gate_all, up_all, part_ref, act_ref, *scratch):
+def exchange(members, picked, inverse, gate_all, up_all, part_ref, act_ref, *scratch):
     stages = stage_count(members)
     me = lax.axis_index(AXIS)
     recv = scratch[:stages]
@@ -316,10 +315,14 @@
         @pl.loop(c * chunk_groups, (c + 1) * chunk_groups)
         def _(g):
             row = pl.multiple_of(g * group_rows, group_rows)
+            scale = inverse[pl.ds(row, group_rows), :]
             for j in range(active):
                 b = picked[g, j]
                 both = jnp.concatenate(
-                    [gate_all[b, pl.ds(row, group_rows), :], up_all[b, pl.ds(row, group_rows), :]],
+                    [
+                        gate_all[b, pl.ds(row, group_rows), :] * scale,
+                        up_all[b, pl.ds(row, group_rows), :] * scale,
+                    ],
                     axis=0,
                 )
                 part_ref[g * active + j] = both.astype(part_ref.dtype)
@@ -425,6 +428,7 @@
             pltpu.VMEM((blocks, rows, blk), jnp.float32),
             pltpu.VMEM((blocks, rows, blk), jnp.float32),
             pltpu.VMEM((pairs,) + tile, jnp.bfloat16),
+            pltpu.VMEM((rows, blk), jnp.float32),
             pltpu.SemaphoreType.DMA((2,)),
         ]
         + buffers(jnp.bfloat16, 0, stages)
@@ -441,7 +445,7 @@
         ),
         name="until_activated",
     )(
-        lengths, picked, queries, residual, norm_gain.reshape(1, width),
+        lengths, picked, queries, residual, norm_gain,
         keys, values, out_weight, gate_weight, up_weight,
     )
 

time: 93.2 us -> 88.3 us (0.947)
  Pallas kernels: 91.8 us -> 88.1 us
  local copies, waits for them, and re-layouts: 1.22 us -> 0 us
    pallas_call x1, Pallas kernels: 84.9 us -> 81.2 us  [until_activated(): pl.pallas_call(functools.partial(layer_kernel, members, rows), out_shape=...]
    reshape x1 -> x0, local copies, waits for them, and re-layouts: 1.22 us -> none  [until_activated(): norm_gain.reshape(1, width)]
where the time goes in v5:
time: 88.3 us; the launch traced here: 88.1 us
  Pallas kernels  88.1 us (100%)
    pallas_call x1, Pallas kernels, until_activated(): pl.pallas_call(functools.partial(layer_kernel, members, rows), out_shape=...  81.2 us
    pallas_call x1, Pallas kernels, project_down(): pl.pallas_call(down_kernel, out_shape=jax.ShapeDtypeStruct((rows, width),...  6.85 us

profile of v5, /device:TPU:0, one launch (start us, length us, event | category | flops | bytes accessed | tf_op | source)
XLA Modules:
  0.0 88.1 jit_solution(15621800929528861487)
XLA Ops:
  0.0 81.2 %until_activated.1 = (f32[128,256]{1,0:T(8,128)}, bf16[256,16,128]{2,1,0:T(8,128)(2,1)}) custom-call(s32[128]{0:T(128)} %lengths.1, s32[16,32]{1,0:T(8,128)} %picked.3, bf16[32,8,128]{2,1,0:T(8,128)(2,1)} %q_ref.1, bf16[128,256]{1,0:T(8,128)(2,1)} %res_ref.1, bf16[256]{0:T(256)(128)(2,1)} %gain_ref.1, bf16[32,1024,128]{2,1,0:T(8,128)(2,1)} %k_hbm.1, ...), custom_call_target="tpu_custom_call" | custom-call | tf_op jit(solution)/shard_map/until_activated/pallas_call | solution.py:403
  81.2 6.9 %project_down.1 = bf16[128,256]{1,0:T(8,128)(2,1)} custom-call(s32[16,32]{1,0:T(8,128)} %picked.3, bf16[256,16,128]{2,1,0:T(8,128)(2,1)} %get-tuple-element.7.act_ref, f32[128,256]{1,0:T(8,128)} %get-tuple-element.8.stream_ref, bf16[14336,256]{1,0:T(8,128)(2,1)} %down_hbm.1), custom_call_target="tpu_custom_call" | custom-call | tf_op jit(solution)/shard_map/project_down/pallas_call | solution.py:68
